TPU v7x, 32 devices: a whole 2x2x4 slice. The times are simulated.
32 devices in a mesh: trc: 4 (over z), lat: 4 (over x, core), lon: 2 (over y).
Axes of the slice: x: 2, y: 2, z: 4, core: 2. Of those that a mesh axis runs over, the one named last changes fastest.
Arguments:
- species_concentrations: float32 [32, 8, 128, 256], P('trc', None, 'lat', 'lon'), may hold values from 0.2 to 4
- zonal_velocity_array: float32 [8, 128, 256], P('trc', 'lat', 'lon'), may hold values from -2.5 to 2.5
- meridional_velocity_array: float32 [8, 128, 256], P('trc', 'lat', 'lon'), may hold values from -2.5 to 2.5
- thermal_anomaly: float32 [8, 128, 256], P('trc', 'lat', 'lon'), may hold values from -6 to 6
- ocean_top_height_grid: float32 [128, 256], P('lat', 'lon'), may hold values from -6 to 6
- water_layer_tally: int32 [128, 256], P('lat', 'lon'), may hold values from 0 to 8
- species_interaction_table: float32 [32, 32], replicated, may hold values from -1 to 1
- species_production_pace: float32 [32], replicated, may hold values from 0.2 to 2
- photon_uptake: float32 [32], replicated, may hold values from 0.01 to 0.1
Outputs:
- updated_tracers: float32 [32, 8, 128, 256], P('trc', None, 'lat', 'lon')
- east_out: float32 [8, 128, 256], P('trc', 'lat', 'lon')
- north_out: float32 [8, 128, 256], P('trc', 'lat', 'lon')
- temperature_out: float32 [8, 128, 256], P('trc', 'lat', 'lon')
- height_out: float32 [128, 256], P('lat', 'lon')
Inputs may be any that keep to these rules, and one draw needn't show every extreme that they name: `water_layer_tally`: the number of wet levels of a column, counted from the surface; cells below it, and whole columns with 0, are land.
All inputs are finite; a program needn't handle non-finite values.
Results may differ from a plain program's by a relative error of at most 0.0003.
Values sent between devices are 32-bit elements; how exact they have to be, the bound alone decides.
No kernel may reach another device: no remote copies, remote signals or barrier semaphores. Data moves between devices by JAX's collectives and lax.ppermute only.
A program may use at most 64 MiB of HBM per device.

v0:
```python
import functools
import math

import jax
import jax.numpy as jnp
from jax import lax
from jax.experimental import pallas as pl
from jax.experimental.pallas import tpu as pltpu
from jax.sharding import PartitionSpec as P

TIME_STEP = 0.1
GRAVITY = 1.0
VISCOSITY = 0.2
BOTTOM_DRAG = 0.05
DEPTH_SCALE = 0.5
CORIOLIS_SCALE = 0.5
COLUMN_DEPTH = 2.0
WATER_ABSORB = 0.2
HALF_LIGHT = 0.5
REACT_STEP = 0.1
WARMING_WEIGHT = 1.0

SUB = 8
LANES = 128
HALO = 4
CORNER = 3
GROUP = 16
F32 = jnp.float32
TOGETHER = 2


def lane_ids():
    return lax.broadcasted_iota(jnp.int32, (SUB, LANES), 1)


def level_ids():
    return lax.broadcasted_iota(jnp.int32, (SUB, LANES), 0)


def roll(x, shift):
    shift = shift % LANES
    return x if shift == 0 else pltpu.roll(x, shift, 1)


def strip_of(rows):
    lane = lane_ids()
    out = None
    for t, value in enumerate(rows):
        rolled = roll(value, GROUP * t + GROUP // 2)
        if out is None:
            out = rolled
        else:
            out = jnp.where(lane // GROUP == t, rolled, out)
    return out


def middle_mask():
    lane = lane_ids() % GROUP
    return (lane >= 4) & (lane < 12)


def pair_up(first, second):
    return jnp.where(middle_mask(), first, roll(second, 8))


def quad_up(a, b, c, d):
    return jnp.where(lane_ids() < 64, pair_up(a, b), roll(pair_up(c, d), 64))


def merge_left(own, got):
    lane = lane_ids() % GROUP
    return jnp.where((lane >= 4) & (lane < 8), got, own)


def merge_right(own, got):
    lane = lane_ids() % GROUP
    return jnp.where((lane >= 8) & (lane < 12), got, own)


def over_levels(row):
    return jnp.broadcast_to(row[0:1, :], (SUB, LANES))


def grant(mib):
    return pltpu.CompilerParams(vmem_limit_bytes=mib << 20)


def pack_tracers_kernel(x_ref, strip_ref, up_ref, down_ref, cols_ref):
    count, rows = x_ref.shape[0], x_ref.shape[1] // SUB
    half = rows // 2

    def row_strip(r):
        return strip_of([x_ref[t, pl.ds(r, SUB, stride=rows), :] for t in range(count)])

    for r in range(half):
        low, high = row_strip(r), row_strip(r + half)
        strip_ref[r] = low
        strip_ref[r + half] = high
        cols_ref[r] = pair_up(low, high)
    for t in range(count):
        for j in range(HALO):
            down_ref[t * HALO + j] = x_ref[t, pl.ds(j, SUB, stride=rows), :]
            up_ref[t * HALO + j] = x_ref[t, pl.ds(rows - HALO + j, SUB, stride=rows), :]


def pack_tracers(x):
    count, rows = x.shape[0], x.shape[1] // SUB
    tile = lambda n: jax.ShapeDtypeStruct((n, SUB, LANES), F32)
    return pl.pallas_call(
        pack_tracers_kernel,
        out_shape=(
            tile(rows),
            tile(count * HALO),
            tile(count * HALO),
            tile(rows // 2),
        ),
        compiler_params=grant(8),
        name="pack_tracers",
    )(x)


def pack_flow_kernel(place_ref, own_ref, *refs):
    peers, rest = refs[:-11], refs[-11:]
    tally_ref, height_ref, tup_ref, tdown_ref, tcols_ref = rest[:5]
    flow_ref, strip_ref, cols_ref, up_ref, down_ref, all_ref = rest[5:]
    rows = tally_ref.shape[0]
    span = own_ref.shape[1]
    place = place_ref[0]
    for k, ref in enumerate((own_ref,) + tuple(peers)):
        base = pl.multiple_of((place ^ k) * span, SUB)
        for f in range(2):
            all_ref[f, pl.ds(base, span), :] = ref[f]
    for src, dst in ((tup_ref, up_ref), (tdown_ref, down_ref), (tcols_ref, cols_ref)):
        dst[0 : src.shape[0]] = src[...]
    nrow, ncol = tup_ref.shape[0], tcols_ref.shape[0]
    level = level_ids()
    tally_all = tally_ref[...].astype(F32)
    pair_all = jnp.minimum(tally_all, pltpu.roll(tally_all, LANES - 1, 1))
    wide = lambda v, r: jnp.broadcast_to(v[r : r + 1, :], (SUB, LANES))
    for r in range(rows):
        tally, height, pair = wide(tally_all, r), wide(height_ref, r), wide(pair_all, r)
        wet = level.astype(F32) < tally
        east = jnp.where(wet, all_ref[0, pl.ds(r, SUB, stride=rows), :], 0.0)
        north = jnp.where(wet, all_ref[1, pl.ds(r, SUB, stride=rows), :], 0.0)
        aux = jnp.where(level == 0, tally, jnp.where(level == 1, height, pair))
        for f, value in enumerate((east, north, aux)):
            flow_ref[f * rows + r] = value
            if r < HALO:
                down_ref[nrow + f * HALO + r] = value
            if r >= rows - HALO:
                up_ref[nrow + f * HALO + r - (rows - HALO)] = value
        strip_ref[r] = strip_of([east, north, aux])
    quarter = rows // 4
    for r in range(quarter):
        cols_ref[ncol + r] = quad_up(*[strip_ref[r + quarter * q] for q in range(4)])


def pack_flow(place, own, peers, tally, height, messages):
    rows = tally.shape[0]
    tile = lambda n: jax.ShapeDtypeStruct((n, SUB, LANES), F32)
    vmem = pl.BlockSpec(memory_space=pltpu.VMEM)
    tup, tdown, tcols = messages
    return pl.pallas_call(
        pack_flow_kernel,
        in_specs=[pl.BlockSpec(memory_space=pltpu.SMEM)] + [vmem] * (3 + len(peers) + len(messages)),
        out_shape=(
            tile(3 * rows),
            tile(rows),
            tile(tcols.shape[0] + rows // 4),
            tile(tup.shape[0] + 3 * HALO),
            tile(tdown.shape[0] + 3 * HALO),
        ),
        scratch_shapes=[pltpu.VMEM((2, SUB * rows, LANES), F32)],
        compiler_params=grant(8),
        name="pack_flow",
    )(place, own, *peers, tally, height, *messages)


def pack_edges_kernel(up_ref, down_ref, out_ref):
    count = up_ref.shape[0] // HALO - 3
    for n, ref in enumerate((up_ref, down_ref)):
        row = lambda f, j: ref[f * HALO + j]
        tracers = [strip_of([row(t, j) for t in range(count)]) for j in range(HALO)]
        flows = [strip_of([row(count + f, j) for f in range(3)]) for j in range(HALO)]
        base = n * CORNER
        for j in range(2):
            out_ref[base + j] = pair_up(tracers[j], tracers[j + 2])
        out_ref[base + 2] = quad_up(*flows)


def pack_edges(up, down):
    return pl.pallas_call(
        pack_edges_kernel,
        out_shape=jax.ShapeDtypeStruct((2 * CORNER, SUB, LANES), F32),
        compiler_params=grant(8),
        name="pack_edges",
    )(up, down)


class Flow:
    def __init__(self, flow_ref, strip_ref, left_ref, right_ref, outer=()):
        self.flow, self.strip = flow_ref, strip_ref
        self.left, self.right = left_ref, right_ref
        self.rows = strip_ref.shape[0]
        self.col_base = left_ref.shape[0] - self.rows // 4
        if outer:
            self.up, self.down, self.corner_left, self.corner_right = outer
            self.row_base = self.up.shape[0] - 3 * HALO

    def corner(self, r):
        return 0 if r < 0 else CORNER

    def row(self, f, r):
        if r < 0:
            return self.up[self.row_base + f * HALO + HALO + r]
        if r >= self.rows:
            return self.down[self.row_base + f * HALO + r - self.rows]
        return self.flow[f * self.rows + r]

    def strips(self, r):
        if 0 <= r < self.rows:
            quarter = self.rows // 4
            q, j = divmod(r, quarter)
            own = self.strip[r]
            left, right = self.left[self.col_base + j], self.right[self.col_base + j]
        else:
            own = strip_of([self.row(f, r) for f in range(3)])
            q = r + HALO if r < 0 else r - self.rows
            at = self.corner(r) + CORNER - 1
            left, right = self.corner_left[at], self.corner_right[at]
        shift = -(8 * (q % 2) + 64 * (q // 2))
        return merge_left(own, roll(left, shift)), merge_right(own, roll(right, shift))


def limited(ahead, behind):
    return jnp.maximum(
        jnp.minimum(ahead, jnp.maximum(behind, 0.0)), jnp.minimum(behind, 0.0)
    )


def face_pair(vel, vel_next, wet):
    a = jnp.where(wet, 0.5 * (vel + vel_next), 0.0)
    size = jnp.abs(a)
    return a, 0.5 * size * (1.0 - size)


def transport_rows(streams, ax_ref, bx_ref, ay_ref, by_ref, first, last):
    states = []
    for load, *_ in streams:
        before, here, after = load(first - 2), load(first - 1), load(first)
        states.append((here, after, limited(after - here, here - before), after - here, None))
    for i in range(first - 1, last):
        for n, (load, store, kind, xo, yo) in enumerate(streams):
            row, nxt, slope, diff, below = states[n]
            far = load(i + 2)
            diff_next = far - nxt
            slope_next = limited(diff_next, diff)
            ay, by = ay_ref[kind, yo + i], by_ref[kind, yo + i]
            positive = ay >= 0.0
            above = ay * jnp.where(positive, row, nxt) + by * jnp.where(positive, slope, slope_next)
            if below is not None:
                ax, bx = ax_ref[kind, xo + i], bx_ref[kind, xo + i]
                east = roll(row, -1)
                dx = east - row
                sx = limited(dx, roll(dx, 1))
                sx_east = roll(sx, -1)
                pos = ax >= 0.0
                fx = ax * jnp.where(pos, row, east) + bx * jnp.where(pos, sx, sx_east)
                store(i, row - (fx - roll(fx, 1)) - (above - below))
            states[n] = (nxt, far, slope_next, diff_next, above)


def select_lanes(moves):
    parts = []
    source = lax.broadcasted_iota(jnp.int32, (LANES, LANES), 0)
    target = lax.broadcasted_iota(jnp.int32, (LANES, LANES), 1)
    for f, d in moves:
        parts.append(jnp.where(source == GROUP * f + target % GROUP + d, 1.0, 0.0))
    return jnp.concatenate(parts, axis=1)


def exact_dot(a, b):
    return jnp.dot(a, b, precision=lax.Precision.HIGHEST, preferred_element_type=F32)


def transport_kernel(
    place_ref, x_ref, strip_ref, flow_ref, fstrip_ref, left_ref, right_ref, *refs, firsts, span, shards
):
    outer, outs, scratch = refs[: -shards - 11], refs[-shards - 11 : -11], refs[-11:]
    ext_ref, ax_ref, bx_ref, ay_ref, by_ref, first_ref, moved_ref, edge_ref, spread_ref, main_ref, shift_ref = scratch
    count, rows = x_ref.shape[0], x_ref.shape[1] // SUB
    half = rows // 2
    place = place_ref[0]
    level = level_ids().astype(F32)
    flow = Flow(flow_ref, fstrip_ref, left_ref, right_ref, outer)
    wide = span + 2 * HALO
    every = [(n, q, first + q) for n, first in enumerate(firsts) for q in range(-HALO, span + HALO)]
    tile_at = lambda n, q: pl.ds((n * wide + q + HALO) * SUB, SUB)

    for n, q, r in every:
        main_ref[tile_at(n, q), :] = flow.row(0, r)
        left, right = flow.strips(r)
        edge_ref[0, tile_at(n, q), :] = left
        edge_ref[1, tile_at(n, q), :] = right
    shift_east = jnp.where(
        lax.broadcasted_iota(jnp.int32, (LANES, LANES), 0)
        == lax.broadcasted_iota(jnp.int32, (LANES, LANES), 1) + 1,
        1.0,
        0.0,
    )
    shift_ref[...] = exact_dot(main_ref[...], shift_east)
    moves = select_lanes(((0, 0), (0, 1), (1, 0), (2, 0), (2, 1)))
    for side in range(2):
        spread_ref[side] = exact_dot(edge_ref[side], moves)

    previous = None
    for n, q, r in every:
        at = tile_at(n, q)
        aux = flow.row(2, r)
        spread = lambda v, i: jnp.broadcast_to(v[i : i + 1, :], (SUB, LANES))
        kinds = [(main_ref[at, :], shift_ref[at, :], flow.row(1, r), spread(aux, 0), spread(aux, 2))]
        for side in range(2):
            east, east_next, north, tally, tally_next = (
                spread_ref[side, at, LANES * j : LANES * (j + 1)] for j in range(5)
            )
            tally, tally_next = spread(tally, 0), spread(tally_next, 0)
            kinds.append((east, east_next, north, tally, jnp.minimum(tally, tally_next)))
        for kind, (east, east_next, north, tally, pair) in enumerate(kinds):
            if -2 <= q < span + 2:
                i = n * (span + 4) + q + 2
                ax_ref[kind, i], bx_ref[kind, i] = face_pair(east, east_next, level < pair)
            if -2 <= q < span + 3:
                i = n * (span + 5) + q + 2
                below, depth = previous[kind]
                ay_ref[kind, i], by_ref[kind, i] = face_pair(
                    below, north, level < jnp.minimum(depth, tally)
                )
        previous = [(k[2], k[3]) for k in kinds]

    for n, q, r in every:
        if r < 0 or r >= rows:
            src = flow.up if r < 0 else flow.down
            j = r + HALO if r < 0 else r - rows
            fields = [src[t * HALO + j] for t in range(count)]
            own = strip_of(fields)
            at = flow.corner(r) + j % 2
            left, right = flow.corner_left[at], flow.corner_right[at]
            swap = j >= 2
        else:
            fields = [x_ref[t, pl.ds(r, SUB, stride=rows), :] for t in range(count)]
            own = strip_ref[r]
            left, right = left_ref[r % half], right_ref[r % half]
            swap = r >= half
        if swap:
            left, right = roll(left, -8), roll(right, -8)
        fields += [merge_left(own, left), merge_right(own, right)]
        for t, value in enumerate(fields):
            ext_ref[t, n * wide + HALO + q] = value

    def some(c, carry):
        before, after = [], []
        for j in range(TOGETHER):
            p = c * TOGETHER + j
            kind = jnp.maximum(p - (count - 1), 0)
            for n in range(len(firsts)):
                xo, yo = n * (span + 4) + 2, n * (span + 5) + 3

                def load_start(i, p=p, n=n):
                    return ext_ref[p, n * wide + HALO + i]

                def store_first(i, value, j=j, xo=xo):
                    first_ref[j, xo + i] = value

                def load_first(i, j=j, xo=xo):
                    return first_ref[j, xo + i]

                def store_moved(i, value, p=p, n=n):
                    moved_ref[p, n * span + i] = value

                before.append((load_start, store_first, kind, xo, yo))
                after.append((load_first, store_moved, kind, xo, yo))
        transport_rows(before, ax_ref, bx_ref, ay_ref, by_ref, -2, span + 2)
        transport_rows(after, ax_ref, bx_ref, ay_ref, by_ref, 0, span)
        return carry

    lax.fori_loop(0, (count + 2) // TOGETHER, some, 0)

    lane = lane_ids()
    edge = (lane < 4) | (lane >= LANES - 4)
    from_right = (lane % GROUP >= 4) & (lane % GROUP < 8)
    share = span * len(firsts) // len(outs)
    for k, out_ref in enumerate(outs):
        base = (place ^ k) * share
        for r in range(share):
            joined = jnp.where(from_right, moved_ref[count + 1, base + r], moved_ref[count, base + r])
            for t in range(count):
                out_ref[t * share + r] = jnp.where(
                    edge, roll(joined, -(GROUP * t + 8)), moved_ref[t, base + r]
                )


def transport(place, shards, x, strip, flow_parts, firsts, span):
    count = x.shape[0]
    vmem = pl.BlockSpec(memory_space=pltpu.VMEM)
    tile = lambda *n: pltpu.VMEM(n + (SUB, LANES), F32)
    flat = lambda *n: pltpu.VMEM(n, F32)
    args = (x, strip) + flow_parts
    pieces = len(firsts)
    wide = (span + 2 * HALO) * pieces
    return pl.pallas_call(
        functools.partial(transport_kernel, firsts=firsts, span=span, shards=shards),
        in_specs=[pl.BlockSpec(memory_space=pltpu.SMEM)] + [vmem] * len(args),
        out_shape=tuple(
            jax.ShapeDtypeStruct((count * span * pieces // shards, SUB, LANES), F32)
            for _ in range(shards)
        ),
        scratch_shapes=[
            tile(count + 2, wide),
            tile(3, (span + 4) * pieces),
            tile(3, (span + 4) * pieces),
            tile(3, (span + 5) * pieces),
            tile(3, (span + 5) * pieces),
            tile(TOGETHER, (span + 4) * pieces),
            tile(count + 2, span * pieces),
            flat(2, wide * SUB, LANES),
            flat(2, wide * SUB, 5 * LANES),
            flat(wide * SUB, LANES),
            flat(wide * SUB, LANES),
        ],
        compiler_params=grant(20),
        name="transport",
    )(place, *args)


def react_kernel(place_ref, table_ref, pace_ref, uptake_ref, surface_ref, tally_ref, *refs, firsts):
    shards = (len(refs) - 3) // 2
    ins, outs = refs[:shards], refs[shards : 2 * shards]
    light_ref, wet_ref, heat_ref = refs[2 * shards :]
    total = pace_ref.shape[0]
    count = total // shards
    share = ins[0].shape[0] // count
    place = place_ref[0]
    level = level_ids()

    for r in range(share):
        at = place * share + r
        span = share * shards // len(firsts)
        row = firsts[0] + at
        for n in range(1, len(firsts)):
            row = jnp.where(at >= n * span, firsts[n] + at - n * span, row)
        tally = jnp.broadcast_to(tally_ref[pl.ds(row, 1), :], (SUB, LANES))
        surface = surface_ref[row]
        wet = jnp.where(level < tally, 1.0, 0.0)
        absorbed = jnp.zeros((SUB, LANES), F32)
        for k, ref in enumerate(ins):
            for t in range(count):
                absorbed = absorbed + uptake_ref[(place ^ k) * count + t] * jnp.abs(ref[t * share + r])
        layer = (COLUMN_DEPTH / SUB) * (WATER_ABSORB + absorbed) * wet
        total_depth = jnp.where(level >= 1, pltpu.roll(layer, 1, 0), 0.0)
        for shift in (1, 2, 4):
            total_depth = total_depth + jnp.where(
                level >= shift, pltpu.roll(total_depth, shift, 0), 0.0
            )
        top = surface * jnp.exp(-total_depth)
        heat_ref[pl.ds(r * SUB, SUB), :] = top * (1.0 - jnp.exp(-layer))
        light_ref[r] = REACT_STEP * wet * (top / (top + HALF_LIGHT))
        wet_ref[r] = REACT_STEP * wet

    block = 4
    for k, out_ref in enumerate(outs):
        for m0 in range(0, count, block):
            dest = [(place ^ k) * count + m0 + j for j in range(block)]
            acc = [[None] * share for _ in range(block)]
            for kk, ref in enumerate(ins):
                for t in range(count):
                    n = (place ^ kk) * count + t
                    values = [ref[t * share + r] for r in range(share)]
                    for j in range(block):
                        c = table_ref[dest[j], n]
                        for r in range(share):
                            term = c * values[r]
                            acc[j][r] = term if acc[j][r] is None else acc[j][r] + term
            for j in range(block):
                pace = pace_ref[dest[j]]
                for r in range(share):
                    own = ins[k][(m0 + j) * share + r]
                    out_ref[(m0 + j) * share + r] = (
                        own + wet_ref[r] * acc[j][r] + pace * (light_ref[r] * own)
                    )
        own_levels = SUB // shards
        out_ref[count * share] = jnp.concatenate(
            [
                heat_ref[pl.ds((place ^ k) * own_levels + q, share, stride=SUB), :]
                for q in range(own_levels)
            ],
            axis=0,
        )


def react(place, table, pace, uptake, surface, tally, blocks, firsts):
    shards = len(blocks)
    share = blocks[0].shape[0] // (pace.shape[0] // shards)
    smem = pl.BlockSpec(memory_space=pltpu.SMEM)
    vmem = pl.BlockSpec(memory_space=pltpu.VMEM)
    assert share * (SUB // shards) == SUB
    return pl.pallas_call(
        functools.partial(react_kernel, firsts=firsts),
        in_specs=[smem] * 5 + [vmem] * (1 + shards),
        out_shape=tuple(
            jax.ShapeDtypeStruct((b.shape[0] + 1, SUB, LANES), F32) for b in blocks
        ),
        scratch_shapes=[
            pltpu.VMEM((share, SUB, LANES), F32),
            pltpu.VMEM((share, SUB, LANES), F32),
            pltpu.VMEM((share * SUB, LANES), F32),
        ],
        compiler_params=grant(8),
        name="react",
    )(place, table, pace, uptake, surface, tally, *blocks)


def finish_kernel(place_ref, thermal_ref, *refs, shards, span):
    ins, (out_ref, temp_ref, cells_ref, heat_ref) = refs[:shards], refs[-4:]
    count = out_ref.shape[0]
    share = span // shards
    own_levels = SUB // shards
    level = level_ids()
    b = pl.program_id(0)

    @pl.when(b == 0)
    def _():
        place = place_ref[0]
        for k, ref in enumerate(ins):
            base = (place ^ k) * share
            for m in range(count):
                for r in range(share):
                    at = pl.multiple_of((m * span + base + r) * SUB, SUB)
                    cells_ref[pl.ds(at, SUB), :] = ref[m * share + r]
            heat = ref[count * share]
            for q in range(own_levels):
                heat_ref[q, place ^ k] = heat if q == 0 else pltpu.roll(heat, SUB - q * share, 0)

    per_tile = SUB // share
    for m in range(count):
        for lev in range(SUB):
            start = b * (SUB * SUB) + (m * span * SUB + lev)
            out_ref[m, lev] = cells_ref[pl.ds(start, SUB, stride=SUB), :]
    for q in range(own_levels):
        heat = heat_ref[q, b * per_tile]
        for n in range(1, per_tile):
            part = pltpu.roll(heat_ref[q, b * per_tile + n], n * share, 0)
            heat = jnp.where(level // share == n, part, heat)
        temp_ref[q] = thermal_ref[q] + WARMING_WEIGHT * heat


def finish(place, thermal, blocks, shape, firsts, span, before):
    shards = len(blocks)
    count, levels, _, cols = shape
    own_levels = thermal.shape[0]
    assert span % SUB == 0 and len(firsts) <= 2 and all(first % SUB == 0 for first in firsts)
    per = span // SUB
    step = per if len(firsts) == 1 else (firsts[1] - firsts[0]) // SUB
    assert len(firsts) == 1 or per == 1
    row_tile = lambda i: firsts[0] // SUB + (i if len(firsts) == 1 else i * step)
    vmem = pl.BlockSpec(memory_space=pltpu.VMEM)
    hold = pl.BlockSpec(memory_space=pl.ANY)
    of_band = lambda *lead: pl.BlockSpec(
        lead + (SUB, cols), lambda i: (0,) * len(lead) + (row_tile(i), 0)
    )
    total = span * len(firsts)
    return pl.pallas_call(
        functools.partial(finish_kernel, shards=shards, span=total),
        grid=(total // SUB,),
        in_specs=[pl.BlockSpec(memory_space=pltpu.SMEM), of_band(own_levels)]
        + [vmem] * shards
        + [hold] * len(before),
        out_specs=(of_band(count, levels), of_band(own_levels)),
        out_shape=(jax.ShapeDtypeStruct(shape, F32), jax.ShapeDtypeStruct(thermal.shape, F32)),
        input_output_aliases={2 + shards + i: i for i in range(len(before))},
        scratch_shapes=[
            pltpu.VMEM((count * total * SUB, LANES), F32),
            pltpu.VMEM((own_levels, shards, SUB, LANES), F32),
        ],
        compiler_params=grant(12),
        name="finish",
    )(place, thermal, *blocks, *before)


def level_sum(x):
    for shift in (4, 2, 1):
        x = x + pltpu.roll(x, shift, 0)
    return x


def momentum_kernel(
    place_ref,
    coriolis_ref,
    inside_ref,
    flow_ref,
    strip_ref,
    left_ref,
    right_ref,
    up_ref,
    down_ref,
    cleft_ref,
    cright_ref,
    east_ref,
    north_ref,
    height_ref,
    a_ref,
    b_ref,
    c_ref,
):
    rows = height_ref.shape[0]
    own_levels = east_ref.shape[0] // rows
    place = place_ref[0]
    lane = lane_ids()
    level = level_ids().astype(F32)
    flow = Flow(flow_ref, strip_ref, left_ref, right_ref, (up_ref, down_ref, cleft_ref, cright_ref))
    for r in range(-2, rows + 2):
        east, north, aux = (flow.row(f, r) for f in range(3))
        left, right = flow.strips(r)
        both = [
            jnp.where(lane < GROUP, roll(left, -GROUP * f), roll(right, GROUP - GROUP * f))
            for f in range(3)
        ]
        for p, (u, v, w) in enumerate(((east, north, aux), both)):
            wet = jnp.where(level < over_levels(w), 1.0, 0.0)
            h = jnp.broadcast_to(w[1:2, :], (SUB, LANES))
            for f, value in enumerate((u, v, h, wet)):
                a_ref[p, f, r + 2] = value

    def substep(src, offset, put, first, last):
        for p in range(2):
            for i in range(first, last):
                g = lambda f, d: src[p, f, i + offset + d]
                u, v, h = g(0, 0), g(1, 0), g(2, 0)
                un, us, vn, vs, hn, hs = g(0, 1), g(0, -1), g(1, 1), g(1, -1), g(2, 1), g(2, -1)
                wet = a_ref[p, 3, i + 2]
                cor = coriolis_ref[i + 2]
                ue, uw, ve, vw, he, hw = (
                    roll(u, -1), roll(u, 1), roll(v, -1), roll(v, 1), roll(h, -1), roll(h, 1),
                )
                div = level_sum(0.5 * (ue - uw) + 0.5 * (vn - vs))
                nu = wet * (
                    u
                    + TIME_STEP
                    * (
                        cor * v
                        - GRAVITY * (0.5 * (he - hw))
                        + VISCOSITY * (un + us + ue + uw - 4.0 * u)
                        - BOTTOM_DRAG * u
                    )
                )
                nv = wet * (
                    v
                    + TIME_STEP
                    * (
                        -cor * u
                        - GRAVITY * (0.5 * (hn - hs))
                        + VISCOSITY * (vn + vs + ve + vw - 4.0 * v)
                        - BOTTOM_DRAG * v
                    )
                )
                nh = h - TIME_STEP * DEPTH_SCALE * div
                put(p, i, nu, nv, nh)

    def put_first(p, i, nu, nv, nh):
        inside = inside_ref[i + 2]
        for f, value in enumerate((nu, nv, nh * inside)):
            b_ref[p, f, i + 1] = value

    def put_second(p, i, nu, nv, nh):
        for f, value in enumerate((nu, nv, nh)):
            c_ref[p, f, pl.ds(i * SUB, SUB), :] = value

    substep(a_ref, 2, put_first, -1, rows + 1)
    substep(b_ref, 1, put_second, 0, rows)

    def joined(f, start):
        lane8 = lax.broadcasted_iota(jnp.int32, (SUB, LANES), 1)
        main = c_ref[0, f, pl.ds(start, SUB, stride=SUB), :]
        edge = c_ref[1, f, pl.ds(start, SUB, stride=SUB), :]
        out = jnp.where(lane8 < 2, roll(edge, -8), main)
        return jnp.where(lane8 >= LANES - 2, roll(edge, LANES - 2 - (GROUP + 6)), out)

    for j in range(rows // SUB):
        for q in range(own_levels):
            lev = place * own_levels + q
            dst = q * rows + j * SUB
            east_ref[dst : dst + SUB, :] = joined(0, j * SUB * SUB + lev)
            north_ref[dst : dst + SUB, :] = joined(1, j * SUB * SUB + lev)
        height_ref[j * SUB : (j + 1) * SUB, :] = joined(2, j * SUB * SUB)


def momentum(place, coriolis, inside, flow_parts, rows, own_levels):
    vmem = pl.BlockSpec(memory_space=pltpu.VMEM)
    args = (coriolis, inside) + flow_parts
    return pl.pallas_call(
        momentum_kernel,
        in_specs=[pl.BlockSpec(memory_space=pltpu.SMEM)] * 3 + [vmem] * len(flow_parts),
        out_shape=(
            jax.ShapeDtypeStruct((own_levels * rows, LANES), F32),
            jax.ShapeDtypeStruct((own_levels * rows, LANES), F32),
            jax.ShapeDtypeStruct((rows, LANES), F32),
        ),
        scratch_shapes=[
            pltpu.VMEM((2, 4, rows + 4, SUB, LANES), F32),
            pltpu.VMEM((2, 3, rows + 2, SUB, LANES), F32),
            pltpu.VMEM((2, 3, rows * SUB, LANES), F32),
        ],
        compiler_params=grant(12),
        name="momentum",
    )(place, *args)


def to_peer(block, k):
    count = lax.axis_size("trc")
    return lax.ppermute(block, "trc", [(i, i ^ k) for i in range(count)])


def exchanged(blocks):
    out = [blocks[0]]
    for k in range(1, len(blocks)):
        out.append(to_peer(blocks[k], k))
    return out


def from_lat(block, step):
    count = lax.axis_size("lat")
    return lax.ppermute(
        block, "lat", [(i, i + step) for i in range(count) if 0 <= i + step < count]
    )


def both_sides(block):
    count = lax.axis_size("lon")
    left = lax.ppermute(block, "lon", [(i, (i + 1) % count) for i in range(count)])
    if count == 2:
        return left, left
    return left, lax.ppermute(block, "lon", [(i, (i - 1) % count) for i in range(count)])


def body(
    species_concentrations,
    zonal_velocity_array,
    meridional_velocity_array,
    thermal_anomaly,
    ocean_top_height_grid,
    water_layer_tally,
    species_interaction_table,
    species_production_pace,
    photon_uptake,
):
    count, levels, rows, cols = species_concentrations.shape
    own_levels = zonal_velocity_array.shape[0]
    shards = lax.axis_size("trc")
    assert levels == SUB and cols == LANES and count * GROUP == LANES and shards & (shards - 1) == 0
    trc_place = lax.axis_index("trc")
    place = trc_place.astype(jnp.int32).reshape(1)
    lat_total = rows * lax.axis_size("lat")
    lat_first = lax.axis_index("lat") * rows
    lat_global = (lat_first + jnp.arange(-2, rows + 2)).astype(F32)
    angle = math.pi * ((lat_global + 0.5) / lat_total - 0.5)
    coriolis = CORIOLIS_SCALE * jnp.sin(angle)
    surface = 1.0 + jnp.cos(angle[2:-2])
    inside = ((lat_global >= 0) & (lat_global < lat_total)).astype(F32)

    x = species_concentrations.reshape(count, levels * rows, cols)
    own = jnp.stack([zonal_velocity_array, meridional_velocity_array]).reshape(
        2, own_levels * rows, cols
    )
    peers = [to_peer(own, k) for k in range(1, shards)]
    strip, *messages = pack_tracers(x)
    flow, fstrip, fcols, fup, fdown = pack_flow(
        place, own, peers, water_layer_tally, ocean_top_height_grid, messages
    )
    left_in, right_in = both_sides(fcols)
    up_in, down_in = from_lat(fup, 1), from_lat(fdown, -1)
    corner = pack_edges(up_in, down_in)
    cleft_in, cright_in = both_sides(corner)
    inner = (flow, fstrip, left_in, right_in)
    outer = (up_in, down_in, cleft_in, cright_in)
    quarter = rows // 4
    bands = (((quarter,), 2 * quarter, inner), ((0, 3 * quarter), quarter, inner + outer))
    blocks = []
    for firsts, span, parts in bands:
        moved = transport(place, shards, x, strip, parts, firsts, span)
        blocks.append(exchanged(moved))
    back = []
    for n, (firsts, span, _) in enumerate(bands):
        reacted = react(
            place,
            species_interaction_table,
            species_production_pace,
            photon_uptake,
            surface,
            water_layer_tally,
            blocks[n],
            firsts,
        )
        back.append(exchanged(reacted))
    late, back[-1][0] = lax.optimization_barrier((place, back[-1][0]))
    east_out, north_out, height_out = momentum(
        late, coriolis, inside, inner + outer, rows, own_levels
    )
    done = ()
    for n, (firsts, span, _) in enumerate(bands):
        done = finish(
            place, thermal_anomaly, back[n], species_concentrations.shape, firsts, span, done
        )
    updated, temperature = done
    vel = (own_levels, rows, cols)
    return (
        updated,
        east_out.reshape(vel),
        north_out.reshape(vel),
        temperature,
        height_out,
    )


def solution(mesh):
    return jax.shard_map(
        body,
        mesh=mesh,
        in_specs=(
            P("trc", None, "lat", "lon"),
            P("trc", "lat", "lon"),
            P("trc", "lat", "lon"),
            P("trc", "lat", "lon"),
            P("lat", "lon"),
            P("lat", "lon"),
            P(),
            P(),
            P(),
        ),
        out_specs=(
            P("trc", None, "lat", "lon"),
            P("trc", "lat", "lon"),
            P("trc", "lat", "lon"),
            P("trc", "lat", "lon"),
            P("lat", "lon"),
        ),
        check_vma=False,
    )
```

profile of v0, /device:TPU:0, one launch (start us, length us, event | category | flops | bytes accessed | tf_op | source)
XLA Modules:
  0.0 88.9 jit_solution(2310740863956356094)
XLA Ops:
  0.7 0.8 pad_maximum_fusion.own_ref
  1.4 5.1 %collective-permute-start.2 = (f32[2,64,128]{2,1,0:T(8,128)S(1)}, f32[2,64,128]{2,1,0:T(8,128)S(1)}, u32[]{:S(2)}, u32[]{:S(2)}) collective-permute-start(f32[2,64,128]{2,1,0:T(8,128)S(1)} %pad_maximum_fusion.own_ref), channel_id=1, source_target_pairs={{0,24},{8,16},{16,8},{24,0},{1,25},{9,17},{17,9},{25,1},{2,26},{10... | collective-permute-start | bytes 196616 | tf_op jit(solution)/shard_map/ppermute | solution.py:719
  6.5 0.6 collective-permute-start
  7.2 1.2 %copy-done = f32[8,8,32,128]{3,2,1,0:T(8,128)S(1)} copy-done((f32[8,8,32,128]{3,2,1,0:T(8,128)S(1)}, f32[8,8,32,128]{3,2,1,0:T(8,128)}, u32[]{:S(2)}) %copy-start) | copy-done | bytes 1048600
  8.4 1.1 %pack_tracers.1 = (f32[32,8,128]{2,1,0:T(8,128)S(1)}, f32[32,8,128]{2,1,0:T(8,128)S(1)}, f32[32,8,128]{2,1,0:T(8,128)S(1)}, f32[16,8,128]{2,1,0:T(8,128)S(1)}) custom-call(f32[8,256,128]{2,1,0:T(8,128)S(1)} %bitcast.6), custom_call_target="tpu_custom_call" | custom-call | tf_op jit(solution)/shard_map/pack_tracers/pallas_call | solution.py:109
  9.5 2.7 %collective-permute-done.1.refs_1_ = f32[2,64,128]{2,1,0:T(8,128)S(1)} collective-permute-done((f32[2,64,128]{2,1,0:T(8,128)S(1)}, f32[2,64,128]{2,1,0:T(8,128)S(1)}, u32[]{:S(2)}, u32[]{:S(2)}) %collective-permute-start.1) | collective-permute-done | bytes 65568 | tf_op jit(solution)/shard_map/ppermute | solution.py:719
  12.5 1.6 %collective-permute-start.4 = (f32[44,8,128]{2,1,0:T(8,128)S(1)}, f32[44,8,128]{2,1,0:T(8,128)S(1)}, u32[]{:S(2)}, u32[]{:S(2)}) collective-permute-start(f32[44,8,128]{2,1,0:T(8,128)S(1)} %get-tuple-element.46), channel_id=1, source_target_pairs={{0,2},{2,4},{4,6},{1,3},{3,5},{5,7},{8,10},{10,12},{12,14},{9,11},... | collective-permute-start | bytes 540680 | tf_op jit(solution)/shard_map/ppermute | solution.py:731
  14.1 1.3 %collective-permute-start.5 = (f32[44,8,128]{2,1,0:T(8,128)S(1)}, f32[44,8,128]{2,1,0:T(8,128)S(1)}, u32[]{:S(2)}, u32[]{:S(2)}) collective-permute-start(f32[44,8,128]{2,1,0:T(8,128)S(1)} %get-tuple-element.47), channel_id=1, source_target_pairs={{2,0},{4,2},{6,4},{3,1},{5,3},{7,5},{10,8},{12,10},{14,12},{11,9},... | collective-permute-start | bytes 540680 | tf_op jit(solution)/shard_map/ppermute | solution.py:731
  15.4 1.7 %collective-permute-start.3 = (f32[24,8,128]{2,1,0:T(8,128)S(1)}, f32[24,8,128]{2,1,0:T(8,128)S(1)}, u32[]{:S(2)}, u32[]{:S(2)}) collective-permute-start(f32[24,8,128]{2,1,0:T(8,128)S(1)} %get-tuple-element.45), channel_id=1, source_target_pairs={{0,1},{1,0},{2,3},{3,2},{4,5},{5,4},{6,7},{7,6},{8,9},{9,8},{10,11... | collective-permute-start | bytes 294920 | tf_op jit(solution)/shard_map/ppermute | solution.py:738
  17.1 3.0 %collective-permute-done.3.left_ref.right_ref = f32[24,8,128]{2,1,0:T(8,128)S(1)} collective-permute-done((f32[24,8,128]{2,1,0:T(8,128)S(1)}, f32[24,8,128]{2,1,0:T(8,128)S(1)}, u32[]{:S(2)}, u32[]{:S(2)}) %collective-permute-start.3) | collective-permute-done | bytes 98336 | tf_op jit(solution)/shard_map/ppermute | solution.py:738
  20.1 5.2 %transport.3 = (f32[32,8,128]{2,1,0:T(8,128)S(1)}, f32[32,8,128]{2,1,0:T(8,128)S(1)}, f32[32,8,128]{2,1,0:T(8,128)S(1)}, f32[32,8,128]{2,1,0:T(8,128)S(1)}) custom-call(s32[1]{0:T(128)} %bitcast.place_ref, f32[8,256,128]{2,1,0:T(8,128)S(1)} %bitcast.7, f32[32,8,128]{2,1,0:T(8,128)S(1)} %get-tuple-element.39.strip_ref, ...), custom_call_target="tpu_custom_call" | custom-call | tf_op jit(solution)/shard_map/transport/pallas_call | solution.py:410
  25.3 0.9 collective-permute-start.13
  26.2 2.2 %collective-permute-start.14 = (f32[32,8,128]{2,1,0:T(8,128)S(1)}, f32[32,8,128]{2,1,0:T(8,128)S(1)}, u32[]{:S(2)}, u32[]{:S(2)}) collective-permute-start(f32[32,8,128]{2,1,0:T(8,128)S(1)} %get-tuple-element.59), channel_id=1, source_target_pairs={{0,16},{8,24},{16,0},{24,8},{1,17},{9,25},{17,1},{25,9},{2,18},{10... | collective-permute-start | bytes 393224 | tf_op jit(solution)/shard_map/ppermute | solution.py:719
  28.4 1.4 %collective-permute-start.15 = (f32[32,8,128]{2,1,0:T(8,128)S(1)}, f32[32,8,128]{2,1,0:T(8,128)S(1)}, u32[]{:S(2)}, u32[]{:S(2)}) collective-permute-start(f32[32,8,128]{2,1,0:T(8,128)S(1)} %get-tuple-element.60), channel_id=1, source_target_pairs={{0,24},{8,16},{16,8},{24,0},{1,25},{9,17},{17,9},{25,1},{2,26},{10... | collective-permute-start | bytes 393224 | tf_op jit(solution)/shard_map/ppermute | solution.py:719
  30.0 1.7 %collective-permute-start.6 = (f32[6,8,128]{2,1,0:T(8,128)S(1)}, f32[6,8,128]{2,1,0:T(8,128)S(1)}, u32[]{:S(2)}, u32[]{:S(2)}) collective-permute-start(f32[6,8,128]{2,1,0:T(8,128)S(1)} %pack_edges.1), channel_id=1, source_target_pairs={{0,1},{1,0},{2,3},{3,2},{4,5},{5,4},{6,7},{7,6},{8,9},{9,8},{10,11... | collective-permute-start | bytes 73736 | tf_op jit(solution)/shard_map/ppermute | solution.py:738
  31.8 1.2 %collective-permute-done.13.refs_1_ = f32[32,8,128]{2,1,0:T(8,128)S(1)} collective-permute-done((f32[32,8,128]{2,1,0:T(8,128)S(1)}, f32[32,8,128]{2,1,0:T(8,128)S(1)}, u32[]{:S(2)}, u32[]{:S(2)}) %collective-permute-start.13) | collective-permute-done | bytes 131104 | tf_op jit(solution)/shard_map/ppermute | solution.py:719
  33.0 5.6 %collective-permute-done.14.refs_2_ = f32[32,8,128]{2,1,0:T(8,128)S(1)} collective-permute-done((f32[32,8,128]{2,1,0:T(8,128)S(1)}, f32[32,8,128]{2,1,0:T(8,128)S(1)}, u32[]{:S(2)}, u32[]{:S(2)}) %collective-permute-start.14) | collective-permute-done | bytes 131104 | tf_op jit(solution)/shard_map/ppermute | solution.py:719
  38.7 2.4 %react.3 = (f32[33,8,128]{2,1,0:T(8,128)S(1)}, f32[33,8,128]{2,1,0:T(8,128)S(1)}, f32[33,8,128]{2,1,0:T(8,128)S(1)}, f32[33,8,128]{2,1,0:T(8,128)S(1)}) custom-call(s32[1]{0:T(128)} %bitcast.place_ref, f32[32,32]{1,0:T(8,128)S(1)} %copy-done.4, f32[32]{0:T(128)S(1)} %copy-done.6, f32[32]{0:T(128)S(1)} %copy-done.7, f32[32]{0:T(128)S(1)} %cosine_add_fusion.surface_ref, ...), custom_call_target="tpu_custom_call" | custom-call | tf_op jit(solution)/shard_map/react/pallas_call | solution.py:506
  41.1 3.4 %collective-permute-start.16 = (f32[33,8,128]{2,1,0:T(8,128)S(1)}, f32[33,8,128]{2,1,0:T(8,128)S(1)}, u32[]{:S(2)}, u32[]{:S(2)}) collective-permute-start(f32[33,8,128]{2,1,0:T(8,128)S(1)} %get-tuple-element.62), channel_id=1, source_target_pairs={{0,8},{8,0},{16,24},{24,16},{1,9},{9,1},{17,25},{25,17},{2,10},{10... | collective-permute-start | bytes 405512 | tf_op jit(solution)/shard_map/ppermute | solution.py:719
  44.6 7.3 %transport.2 = (f32[32,8,128]{2,1,0:T(8,128)S(1)}, f32[32,8,128]{2,1,0:T(8,128)S(1)}, f32[32,8,128]{2,1,0:T(8,128)S(1)}, f32[32,8,128]{2,1,0:T(8,128)S(1)}) custom-call(s32[1]{0:T(128)} %bitcast.place_ref, f32[8,256,128]{2,1,0:T(8,128)S(1)} %bitcast.8, f32[32,8,128]{2,1,0:T(8,128)S(1)} %get-tuple-element.39.strip_ref, ...), custom_call_target="tpu_custom_call" | custom-call | tf_op jit(solution)/shard_map/transport/pallas_call | solution.py:410
  52.0 2.5 %collective-permute-start.8 = (f32[32,8,128]{2,1,0:T(8,128)S(1)}, f32[32,8,128]{2,1,0:T(8,128)S(1)}, u32[]{:S(2)}, u32[]{:S(2)}) collective-permute-start(f32[32,8,128]{2,1,0:T(8,128)S(1)} %get-tuple-element.50), channel_id=1, source_target_pairs={{0,16},{8,24},{16,0},{24,8},{1,17},{9,25},{17,1},{25,9},{2,18},{10... | collective-permute-start | bytes 393224 | tf_op jit(solution)/shard_map/ppermute | solution.py:719
  54.5 1.9 %collective-permute-start.9 = (f32[32,8,128]{2,1,0:T(8,128)S(1)}, f32[32,8,128]{2,1,0:T(8,128)S(1)}, u32[]{:S(2)}, u32[]{:S(2)}) collective-permute-start(f32[32,8,128]{2,1,0:T(8,128)S(1)} %get-tuple-element.51), channel_id=1, source_target_pairs={{0,24},{8,16},{16,8},{24,0},{1,25},{9,17},{17,9},{25,1},{2,26},{10... | collective-permute-start | bytes 393224 | tf_op jit(solution)/shard_map/ppermute | solution.py:719
  56.4 3.0 %collective-permute-done.7.refs_1_ = f32[32,8,128]{2,1,0:T(8,128)S(1)} collective-permute-done((f32[32,8,128]{2,1,0:T(8,128)S(1)}, f32[32,8,128]{2,1,0:T(8,128)S(1)}, u32[]{:S(2)}, u32[]{:S(2)}) %collective-permute-start.7) | collective-permute-done | bytes 131104 | tf_op jit(solution)/shard_map/ppermute | solution.py:719
  59.3 1.9 %collective-permute-start.18 = (f32[33,8,128]{2,1,0:T(8,128)S(1)}, f32[33,8,128]{2,1,0:T(8,128)S(1)}, u32[]{:S(2)}, u32[]{:S(2)}) collective-permute-start(f32[33,8,128]{2,1,0:T(8,128)S(1)} %get-tuple-element.64), channel_id=1, source_target_pairs={{0,24},{8,16},{16,8},{24,0},{1,25},{9,17},{17,9},{25,1},{2,26},{10... | collective-permute-start | bytes 405512 | tf_op jit(solution)/shard_map/ppermute | solution.py:719
  61.3 9.5 %collective-permute-done.8.refs_2_ = f32[32,8,128]{2,1,0:T(8,128)S(1)} collective-permute-done((f32[32,8,128]{2,1,0:T(8,128)S(1)}, f32[32,8,128]{2,1,0:T(8,128)S(1)}, u32[]{:S(2)}, u32[]{:S(2)}) %collective-permute-start.8) | collective-permute-done | bytes 131104 | tf_op jit(solution)/shard_map/ppermute | solution.py:719
  70.8 2.4 %react.2 = (f32[33,8,128]{2,1,0:T(8,128)S(1)}, f32[33,8,128]{2,1,0:T(8,128)S(1)}, f32[33,8,128]{2,1,0:T(8,128)S(1)}, f32[33,8,128]{2,1,0:T(8,128)S(1)}) custom-call(s32[1]{0:T(128)} %bitcast.place_ref, f32[32,32]{1,0:T(8,128)S(1)} %copy-done.4, f32[32]{0:T(128)S(1)} %copy-done.6, f32[32]{0:T(128)S(1)} %copy-done.7, f32[32]{0:T(128)S(1)} %cosine_add_fusion.surface_ref, ...), custom_call_target="tpu_custom_call" | custom-call | tf_op jit(solution)/shard_map/react/pallas_call | solution.py:506
  73.2 3.4 %collective-permute-start.10 = (f32[33,8,128]{2,1,0:T(8,128)S(1)}, f32[33,8,128]{2,1,0:T(8,128)S(1)}, u32[]{:S(2)}, u32[]{:S(2)}) collective-permute-start(f32[33,8,128]{2,1,0:T(8,128)S(1)} %get-tuple-element.54), channel_id=1, source_target_pairs={{0,8},{8,0},{16,24},{24,16},{1,9},{9,1},{17,25},{25,17},{2,10},{10... | collective-permute-start | bytes 405512 | tf_op jit(solution)/shard_map/ppermute | solution.py:719
  77.2 1.9 %collective-permute-start.12 = (f32[33,8,128]{2,1,0:T(8,128)S(1)}, f32[33,8,128]{2,1,0:T(8,128)S(1)}, u32[]{:S(2)}, u32[]{:S(2)}) collective-permute-start(f32[33,8,128]{2,1,0:T(8,128)S(1)} %get-tuple-element.56), channel_id=1, source_target_pairs={{0,24},{8,16},{16,8},{24,0},{1,25},{9,17},{17,9},{25,1},{2,26},{10... | collective-permute-start | bytes 405512 | tf_op jit(solution)/shard_map/ppermute | solution.py:719
  79.1 4.0 %momentum.1 = (f32[64,128]{1,0:T(8,128)}, f32[64,128]{1,0:T(8,128)}, f32[32,128]{1,0:T(8,128)}) custom-call(s32[1]{0:T(128)} %bitcast.place_ref, f32[36]{0:T(128)S(1)} %sine_multiply_fusion.coriolis_ref, f32[36]{0:T(128)S(1)} %and_convert_fusion.inside_ref, f32[96,8,128]{2,1,0:T(8,128)S(1)} %get-tuple-element.43.flow_ref, ...), custom_call_target="tpu_custom_call" | custom-call | tf_op jit(solution)/shard_map/momentum/pallas_call | solution.py:699
  83.2 0.9 %finish.2 = (f32[8,8,32,128]{3,2,1,0:T(8,128)}, f32[2,32,128]{2,1,0:T(8,128)}) custom-call(s32[1]{0:T(128)} %bitcast.place_ref, f32[2,32,128]{2,1,0:T(8,128)S(1)} %copy-done.3, f32[33,8,128]{2,1,0:T(8,128)S(1)} %get-tuple-element.61.refs_0_, f32[33,8,128]{2,1,0:T(8,128)S(1)} %collective-permute-done.16.refs_1_, ...), custom_call_target="tpu_custom_call" | custom-call | tf_op jit(solution)/shard_map/finish/pallas_call | solution.py:571
  84.1 3.9 %collective-permute-done.11.refs_2_ = f32[33,8,128]{2,1,0:T(8,128)S(1)} collective-permute-done((f32[33,8,128]{2,1,0:T(8,128)S(1)}, f32[33,8,128]{2,1,0:T(8,128)S(1)}, u32[]{:S(2)}, u32[]{:S(2)}) %collective-permute-start.11) | collective-permute-done | bytes 135200 | tf_op jit(solution)/shard_map/ppermute | solution.py:719
  88.0 0.9 %finish.3 = (f32[8,8,32,128]{3,2,1,0:T(8,128)}, f32[2,32,128]{2,1,0:T(8,128)}) custom-call(s32[1]{0:T(128)} %bitcast.place_ref, f32[2,32,128]{2,1,0:T(8,128)S(1)} %copy-done.3, f32[33,8,128]{2,1,0:T(8,128)S(1)} %get-tuple-element.53.refs_0_, f32[33,8,128]{2,1,0:T(8,128)S(1)} %collective-permute-done.10.refs_1_, ...), custom_call_target="tpu_custom_call", output_to_operand_aliasing={{0}: (6, {}), {1}: (7, {})} | custom-call | tf_op jit(solution)/shard_map/finish/pallas_call | solution.py:571
  (37 shorter events, 1.5 us)
Async XLA Ops:
  0.6 11.5 %copy-start.2 = (s32[32,128]{1,0:T(8,128)S(1)}, s32[32,128]{1,0:T(8,128)}, u32[]{:S(2)}) copy-start(s32[32,128]{1,0:T(8,128)} %tally_ref.3) | copy-start | bytes 49156
  0.6 11.5 %copy-start.5 = (f32[32,128]{1,0:T(8,128)S(1)}, f32[32,128]{1,0:T(8,128)}, u32[]{:S(2)}) copy-start(f32[32,128]{1,0:T(8,128)} %refs_4_.1) | copy-start | bytes 49156
  1.4 8.0 %collective-permute-start.2 = (f32[2,64,128]{2,1,0:T(8,128)S(1)}, f32[2,64,128]{2,1,0:T(8,128)S(1)}, u32[]{:S(2)}, u32[]{:S(2)}) collective-permute-start(f32[2,64,128]{2,1,0:T(8,128)S(1)} %pad_maximum_fusion.own_ref), channel_id=1, source_target_pairs={{0,24},{8,16},{16,8},{24,0},{1,25},{9,17},{17,9},{25,1},{2,26},{10... | collective-permute-start | bytes 196616 | tf_op jit(solution)/shard_map/ppermute | solution.py:719
  6.5 5.6 %collective-permute-start.1 = (f32[2,64,128]{2,1,0:T(8,128)S(1)}, f32[2,64,128]{2,1,0:T(8,128)S(1)}, u32[]{:S(2)}, u32[]{:S(2)}) collective-permute-start(f32[2,64,128]{2,1,0:T(8,128)S(1)} %pad_maximum_fusion.own_ref), channel_id=1, source_target_pairs={{0,16},{8,24},{16,0},{24,8},{1,17},{9,25},{17,1},{25,9},{2,18},{10... | collective-permute-start | bytes 196616 | tf_op jit(solution)/shard_map/ppermute | solution.py:719
  6.5 5.6 %collective-permute-start = (f32[2,64,128]{2,1,0:T(8,128)S(1)}, f32[2,64,128]{2,1,0:T(8,128)S(1)}, u32[]{:S(2)}, u32[]{:S(2)}) collective-permute-start(f32[2,64,128]{2,1,0:T(8,128)S(1)} %pad_maximum_fusion.own_ref), channel_id=1, source_target_pairs={{0,8},{8,0},{16,24},{24,16},{1,9},{9,1},{17,25},{25,17},{2,10},{10... | collective-permute-start | bytes 196616 | tf_op jit(solution)/shard_map/ppermute | solution.py:719
  7.2 1.2 %copy-start = (f32[8,8,32,128]{3,2,1,0:T(8,128)S(1)}, f32[8,8,32,128]{3,2,1,0:T(8,128)}, u32[]{:S(2)}) copy-start(f32[8,8,32,128]{3,2,1,0:T(8,128)} %param.9) | copy-start | bytes 3145732
  8.4 11.7 %copy-start.1 = (f32[8,8,32,128]{3,2,1,0:T(8,128)S(1)}, f32[8,8,32,128]{3,2,1,0:T(8,128)}, u32[]{:S(2)}) copy-start(f32[8,8,32,128]{3,2,1,0:T(8,128)} %param.9) | copy-start | bytes 3145732
  12.5 17.3 %collective-permute-start.4 = (f32[44,8,128]{2,1,0:T(8,128)S(1)}, f32[44,8,128]{2,1,0:T(8,128)S(1)}, u32[]{:S(2)}, u32[]{:S(2)}) collective-permute-start(f32[44,8,128]{2,1,0:T(8,128)S(1)} %get-tuple-element.46), channel_id=1, source_target_pairs={{0,2},{2,4},{4,6},{1,3},{3,5},{5,7},{8,10},{10,12},{12,14},{9,11},... | collective-permute-start | bytes 540680 | tf_op jit(solution)/shard_map/ppermute | solution.py:731
  14.1 15.7 %collective-permute-start.5 = (f32[44,8,128]{2,1,0:T(8,128)S(1)}, f32[44,8,128]{2,1,0:T(8,128)S(1)}, u32[]{:S(2)}, u32[]{:S(2)}) collective-permute-start(f32[44,8,128]{2,1,0:T(8,128)S(1)} %get-tuple-element.47), channel_id=1, source_target_pairs={{2,0},{4,2},{6,4},{3,1},{5,3},{7,5},{10,8},{12,10},{14,12},{11,9},... | collective-permute-start | bytes 540680 | tf_op jit(solution)/shard_map/ppermute | solution.py:731
  15.4 4.7 %collective-permute-start.3 = (f32[24,8,128]{2,1,0:T(8,128)S(1)}, f32[24,8,128]{2,1,0:T(8,128)S(1)}, u32[]{:S(2)}, u32[]{:S(2)}) collective-permute-start(f32[24,8,128]{2,1,0:T(8,128)S(1)} %get-tuple-element.45), channel_id=1, source_target_pairs={{0,1},{1,0},{2,3},{3,2},{4,5},{5,4},{6,7},{7,6},{8,9},{9,8},{10,11... | collective-permute-start | bytes 294920 | tf_op jit(solution)/shard_map/ppermute | solution.py:738
  25.3 7.7 %collective-permute-start.13 = (f32[32,8,128]{2,1,0:T(8,128)S(1)}, f32[32,8,128]{2,1,0:T(8,128)S(1)}, u32[]{:S(2)}, u32[]{:S(2)}) collective-permute-start(f32[32,8,128]{2,1,0:T(8,128)S(1)} %get-tuple-element.58), channel_id=1, source_target_pairs={{0,8},{8,0},{16,24},{24,16},{1,9},{9,1},{17,25},{25,17},{2,10},{10... | collective-permute-start | bytes 393224 | tf_op jit(solution)/shard_map/ppermute | solution.py:719
  26.2 12.5 %collective-permute-start.14 = (f32[32,8,128]{2,1,0:T(8,128)S(1)}, f32[32,8,128]{2,1,0:T(8,128)S(1)}, u32[]{:S(2)}, u32[]{:S(2)}) collective-permute-start(f32[32,8,128]{2,1,0:T(8,128)S(1)} %get-tuple-element.59), channel_id=1, source_target_pairs={{0,16},{8,24},{16,0},{24,8},{1,17},{9,25},{17,1},{25,9},{2,18},{10... | collective-permute-start | bytes 393224 | tf_op jit(solution)/shard_map/ppermute | solution.py:719
  28.4 10.3 %copy-start.4 = (f32[32,32]{1,0:T(8,128)S(1)}, f32[32,32]{1,0:T(8,128)}, u32[]{:S(2)}) copy-start(f32[32,32]{1,0:T(8,128)} %table_ref.3) | copy-start | bytes 12292
  28.4 10.3 %collective-permute-start.15 = (f32[32,8,128]{2,1,0:T(8,128)S(1)}, f32[32,8,128]{2,1,0:T(8,128)S(1)}, u32[]{:S(2)}, u32[]{:S(2)}) collective-permute-start(f32[32,8,128]{2,1,0:T(8,128)S(1)} %get-tuple-element.60), channel_id=1, source_target_pairs={{0,24},{8,16},{16,8},{24,0},{1,25},{9,17},{17,9},{25,1},{2,26},{10... | collective-permute-start | bytes 393224 | tf_op jit(solution)/shard_map/ppermute | solution.py:719
  30.0 14.5 %collective-permute-start.6 = (f32[6,8,128]{2,1,0:T(8,128)S(1)}, f32[6,8,128]{2,1,0:T(8,128)S(1)}, u32[]{:S(2)}, u32[]{:S(2)}) collective-permute-start(f32[6,8,128]{2,1,0:T(8,128)S(1)} %pack_edges.1), channel_id=1, source_target_pairs={{0,1},{1,0},{2,3},{3,2},{4,5},{5,4},{6,7},{7,6},{8,9},{9,8},{10,11... | collective-permute-start | bytes 73736 | tf_op jit(solution)/shard_map/ppermute | solution.py:738
  31.8 6.9 %copy-start.6 = (f32[32]{0:T(128)S(1)}, f32[32]{0:T(128)}, u32[]{:S(2)}) copy-start(f32[32]{0:T(128)} %pace_ref.3) | copy-start | bytes 388
  31.8 6.9 %copy-start.7 = (f32[32]{0:T(128)S(1)}, f32[32]{0:T(128)}, u32[]{:S(2)}) copy-start(f32[32]{0:T(128)} %uptake_ref.3) | copy-start | bytes 388
  41.1 36.1 %collective-permute-start.16 = (f32[33,8,128]{2,1,0:T(8,128)S(1)}, f32[33,8,128]{2,1,0:T(8,128)S(1)}, u32[]{:S(2)}, u32[]{:S(2)}) collective-permute-start(f32[33,8,128]{2,1,0:T(8,128)S(1)} %get-tuple-element.62), channel_id=1, source_target_pairs={{0,8},{8,0},{16,24},{24,16},{1,9},{9,1},{17,25},{25,17},{2,10},{10... | collective-permute-start | bytes 405512 | tf_op jit(solution)/shard_map/ppermute | solution.py:719
  51.9 7.4 %collective-permute-start.7 = (f32[32,8,128]{2,1,0:T(8,128)S(1)}, f32[32,8,128]{2,1,0:T(8,128)S(1)}, u32[]{:S(2)}, u32[]{:S(2)}) collective-permute-start(f32[32,8,128]{2,1,0:T(8,128)S(1)} %get-tuple-element.49), channel_id=1, source_target_pairs={{0,8},{8,0},{16,24},{24,16},{1,9},{9,1},{17,25},{25,17},{2,10},{10... | collective-permute-start | bytes 393224 | tf_op jit(solution)/shard_map/ppermute | solution.py:719
  52.0 18.8 %collective-permute-start.8 = (f32[32,8,128]{2,1,0:T(8,128)S(1)}, f32[32,8,128]{2,1,0:T(8,128)S(1)}, u32[]{:S(2)}, u32[]{:S(2)}) collective-permute-start(f32[32,8,128]{2,1,0:T(8,128)S(1)} %get-tuple-element.50), channel_id=1, source_target_pairs={{0,16},{8,24},{16,0},{24,8},{1,17},{9,25},{17,1},{25,9},{2,18},{10... | collective-permute-start | bytes 393224 | tf_op jit(solution)/shard_map/ppermute | solution.py:719
  54.5 16.3 %collective-permute-start.9 = (f32[32,8,128]{2,1,0:T(8,128)S(1)}, f32[32,8,128]{2,1,0:T(8,128)S(1)}, u32[]{:S(2)}, u32[]{:S(2)}) collective-permute-start(f32[32,8,128]{2,1,0:T(8,128)S(1)} %get-tuple-element.51), channel_id=1, source_target_pairs={{0,24},{8,16},{16,8},{24,0},{1,25},{9,17},{17,9},{25,1},{2,26},{10... | collective-permute-start | bytes 393224 | tf_op jit(solution)/shard_map/ppermute | solution.py:719
  56.4 26.8 %collective-permute-start.17 = (f32[33,8,128]{2,1,0:T(8,128)S(1)}, f32[33,8,128]{2,1,0:T(8,128)S(1)}, u32[]{:S(2)}, u32[]{:S(2)}) collective-permute-start(f32[33,8,128]{2,1,0:T(8,128)S(1)} %get-tuple-element.63), channel_id=1, source_target_pairs={{0,16},{8,24},{16,0},{24,8},{1,17},{9,25},{17,1},{25,9},{2,18},{10... | collective-permute-start | bytes 405512 | tf_op jit(solution)/shard_map/ppermute | solution.py:719
  59.3 23.8 %collective-permute-start.18 = (f32[33,8,128]{2,1,0:T(8,128)S(1)}, f32[33,8,128]{2,1,0:T(8,128)S(1)}, u32[]{:S(2)}, u32[]{:S(2)}) collective-permute-start(f32[33,8,128]{2,1,0:T(8,128)S(1)} %get-tuple-element.64), channel_id=1, source_target_pairs={{0,24},{8,16},{16,8},{24,0},{1,25},{9,17},{17,9},{25,1},{2,26},{10... | collective-permute-start | bytes 405512 | tf_op jit(solution)/shard_map/ppermute | solution.py:719
  73.2 11.0 %collective-permute-start.10 = (f32[33,8,128]{2,1,0:T(8,128)S(1)}, f32[33,8,128]{2,1,0:T(8,128)S(1)}, u32[]{:S(2)}, u32[]{:S(2)}) collective-permute-start(f32[33,8,128]{2,1,0:T(8,128)S(1)} %get-tuple-element.54), channel_id=1, source_target_pairs={{0,8},{8,0},{16,24},{24,16},{1,9},{9,1},{17,25},{25,17},{2,10},{10... | collective-permute-start | bytes 405512 | tf_op jit(solution)/shard_map/ppermute | solution.py:719
  76.6 11.4 %collective-permute-start.11 = (f32[33,8,128]{2,1,0:T(8,128)S(1)}, f32[33,8,128]{2,1,0:T(8,128)S(1)}, u32[]{:S(2)}, u32[]{:S(2)}) collective-permute-start(f32[33,8,128]{2,1,0:T(8,128)S(1)} %get-tuple-element.55), channel_id=1, source_target_pairs={{0,16},{8,24},{16,0},{24,8},{1,17},{9,25},{17,1},{25,9},{2,18},{10... | collective-permute-start | bytes 405512 | tf_op jit(solution)/shard_map/ppermute | solution.py:719
  77.2 10.8 %collective-permute-start.12 = (f32[33,8,128]{2,1,0:T(8,128)S(1)}, f32[33,8,128]{2,1,0:T(8,128)S(1)}, u32[]{:S(2)}, u32[]{:S(2)}) collective-permute-start(f32[33,8,128]{2,1,0:T(8,128)S(1)} %get-tuple-element.56), channel_id=1, source_target_pairs={{0,24},{8,16},{16,8},{24,0},{1,25},{9,17},{17,9},{25,1},{2,26},{10... | collective-permute-start | bytes 405512 | tf_op jit(solution)/shard_map/ppermute | solution.py:719
  79.1 4.1 %copy-start.3 = (f32[2,32,128]{2,1,0:T(8,128)S(1)}, f32[2,32,128]{2,1,0:T(8,128)}, u32[]{:S(2)}) copy-start(f32[2,32,128]{2,1,0:T(8,128)} %thermal_ref.3) | copy-start | bytes 98308
where the time goes:
time: 89.2 us; the launch traced here: 88.9 us
  starting transfers between devices  32.1 us (36%)
  waiting for transfers between devices  28.9 us (32%)
  Pallas kernels  24.9 us (28%)
  local copies, waits for them, and re-layouts  1.26 us (1%)
  other arithmetic  0.97 us (1%)
    ppermute x15, waiting for transfers between devices, to_peer(): return lax.ppermute(block, 'trc', [(i, i ^ k) for i in range(count)])  25.9 us
    ppermute x15, starting transfers between devices, to_peer(): return lax.ppermute(block, 'trc', [(i, i ^ k) for i in range(count)])  25.8 us
    pallas_call x2, Pallas kernels, transport(): pl.pallas_call(functools.partial(transport_kernel, firsts=firsts, span=sp...  12.6 us
    pallas_call x2, Pallas kernels, react(): pl.pallas_call(functools.partial(react_kernel, firsts=firsts), in_specs=[...  4.81 us
    pallas_call x1, Pallas kernels, momentum(): pl.pallas_call(momentum_kernel, in_specs=[pl.BlockSpec(memory_space=pltpu...  4.04 us
    ppermute x2, starting transfers between devices, both_sides(): lax.ppermute(block, 'lon', [(i, (i + 1) % count) for i in range(count)])  3.4 us
    ppermute x2, waiting for transfers between devices, both_sides(): lax.ppermute(block, 'lon', [(i, (i + 1) % count) for i in range(count)])  2.97 us
    ppermute x2, starting transfers between devices, from_lat(): lax.ppermute(block, 'lat', [(i, i + step) for i in range(count) if 0 <= i...  2.87 us
  transfers between devices with their start and end apart: 19, of which 7 were waited for; matrix products, arithmetic and copies ran while one was open for 0% of the time, Pallas kernels for 27%

commit v1 on v0

--- a/solution.py
+++ b/solution.py
@@ -26,7 +26,6 @@
 CORNER = 3
 GROUP = 16
 F32 = jnp.float32
-TOGETHER = 2
 
 
 def lane_ids():
@@ -75,6 +74,13 @@
 def merge_right(own, got):
     lane = lane_ids() % GROUP
     return jnp.where((lane >= 8) & (lane < 12), got, own)
+
+
+def band_row(firsts, span, at):
+    row = firsts[0] + at
+    for n in range(1, len(firsts)):
+        row = jnp.where(at >= n * span, firsts[n] + at - n * span, row)
+    return row
 
 
 def over_levels(row):
@@ -284,7 +290,7 @@
 
 
 def transport_kernel(
-    place_ref, x_ref, strip_ref, flow_ref, fstrip_ref, left_ref, right_ref, *refs, firsts, span, shards
+    place_ref, x_ref, strip_ref, flow_ref, fstrip_ref, left_ref, right_ref, *refs, firsts, span, shards, together
 ):
     outer, outs, scratch = refs[: -shards - 11], refs[-shards - 11 : -11], refs[-11:]
     ext_ref, ax_ref, bx_ref, ay_ref, by_ref, first_ref, moved_ref, edge_ref, spread_ref, main_ref, shift_ref = scratch
@@ -359,8 +365,8 @@
 
     def some(c, carry):
         before, after = [], []
-        for j in range(TOGETHER):
-            p = c * TOGETHER + j
+        for j in range(together):
+            p = c * together + j
             kind = jnp.maximum(p - (count - 1), 0)
             for n in range(len(firsts)):
                 xo, yo = n * (span + 4) + 2, n * (span + 5) + 3
@@ -383,7 +389,7 @@
         transport_rows(after, ax_ref, bx_ref, ay_ref, by_ref, 0, span)
         return carry
 
-    lax.fori_loop(0, (count + 2) // TOGETHER, some, 0)
+    lax.fori_loop(0, (count + 2) // together, some, 0)
 
     lane = lane_ids()
     edge = (lane < 4) | (lane >= LANES - 4)
@@ -399,7 +405,7 @@
                 )
 
 
-def transport(place, shards, x, strip, flow_parts, firsts, span):
+def transport(place, shards, x, strip, flow_parts, firsts, span, together):
     count = x.shape[0]
     vmem = pl.BlockSpec(memory_space=pltpu.VMEM)
     tile = lambda *n: pltpu.VMEM(n + (SUB, LANES), F32)
@@ -408,7 +414,7 @@
     pieces = len(firsts)
     wide = (span + 2 * HALO) * pieces
     return pl.pallas_call(
-        functools.partial(transport_kernel, firsts=firsts, span=span, shards=shards),
+        functools.partial(transport_kernel, firsts=firsts, span=span, shards=shards, together=together),
         in_specs=[pl.BlockSpec(memory_space=pltpu.SMEM)] + [vmem] * len(args),
         out_shape=tuple(
             jax.ShapeDtypeStruct((count * span * pieces // shards, SUB, LANES), F32)
@@ -420,7 +426,7 @@
             tile(3, (span + 4) * pieces),
             tile(3, (span + 5) * pieces),
             tile(3, (span + 5) * pieces),
-            tile(TOGETHER, (span + 4) * pieces),
+            tile(together, (span + 4) * pieces),
             tile(count + 2, span * pieces),
             flat(2, wide * SUB, LANES),
             flat(2, wide * SUB, 5 * LANES),
@@ -441,13 +447,10 @@
     share = ins[0].shape[0] // count
     place = place_ref[0]
     level = level_ids()
+    heat_ref[...] = jnp.zeros_like(heat_ref)
 
     for r in range(share):
-        at = place * share + r
-        span = share * shards // len(firsts)
-        row = firsts[0] + at
-        for n in range(1, len(firsts)):
-            row = jnp.where(at >= n * span, firsts[n] + at - n * span, row)
+        row = band_row(firsts, share * shards // len(firsts), place * share + r)
         tally = jnp.broadcast_to(tally_ref[pl.ds(row, 1), :], (SUB, LANES))
         surface = surface_ref[row]
         wet = jnp.where(level < tally, 1.0, 0.0)
@@ -488,13 +491,9 @@
                         own + wet_ref[r] * acc[j][r] + pace * (light_ref[r] * own)
                     )
         own_levels = SUB // shards
-        out_ref[count * share] = jnp.concatenate(
-            [
-                heat_ref[pl.ds((place ^ k) * own_levels + q, share, stride=SUB), :]
-                for q in range(own_levels)
-            ],
-            axis=0,
-        )
+        for q in range(own_levels):
+            level_at = (place ^ k) * own_levels + q
+            out_ref[count * share + q] = heat_ref[pl.ds(level_at, SUB, stride=SUB), :]
 
 
 def react(place, table, pace, uptake, surface, tally, blocks, firsts):
@@ -502,88 +501,63 @@
     share = blocks[0].shape[0] // (pace.shape[0] // shards)
     smem = pl.BlockSpec(memory_space=pltpu.SMEM)
     vmem = pl.BlockSpec(memory_space=pltpu.VMEM)
-    assert share * (SUB // shards) == SUB
+    assert share <= SUB
     return pl.pallas_call(
         functools.partial(react_kernel, firsts=firsts),
         in_specs=[smem] * 5 + [vmem] * (1 + shards),
         out_shape=tuple(
-            jax.ShapeDtypeStruct((b.shape[0] + 1, SUB, LANES), F32) for b in blocks
+            jax.ShapeDtypeStruct((b.shape[0] + SUB // shards, SUB, LANES), F32) for b in blocks
         ),
         scratch_shapes=[
             pltpu.VMEM((share, SUB, LANES), F32),
             pltpu.VMEM((share, SUB, LANES), F32),
-            pltpu.VMEM((share * SUB, LANES), F32),
+            pltpu.VMEM((SUB * SUB, LANES), F32),
         ],
         compiler_params=grant(8),
         name="react",
     )(place, table, pace, uptake, surface, tally, *blocks)
 
 
-def finish_kernel(place_ref, thermal_ref, *refs, shards, span):
-    ins, (out_ref, temp_ref, cells_ref, heat_ref) = refs[:shards], refs[-4:]
-    count = out_ref.shape[0]
-    share = span // shards
+def finish_kernel(place_ref, thermal_ref, *refs, bands, shards):
+    *ins, out_ref, temp_ref, cells_ref = refs
+    count, _, rows, _ = out_ref.shape
     own_levels = SUB // shards
-    level = level_ids()
-    b = pl.program_id(0)
-
-    @pl.when(b == 0)
-    def _():
-        place = place_ref[0]
-        for k, ref in enumerate(ins):
-            base = (place ^ k) * share
-            for m in range(count):
-                for r in range(share):
-                    at = pl.multiple_of((m * span + base + r) * SUB, SUB)
+    place = place_ref[0]
+    for n, (firsts, span) in enumerate(bands):
+        share = span * len(firsts) // shards
+        for k, ref in enumerate(ins[n * shards : (n + 1) * shards]):
+            for r in range(share):
+                row = band_row(firsts, span, (place ^ k) * share + r)
+                for m in range(count):
+                    at = pl.multiple_of((m * rows + row) * SUB, SUB)
                     cells_ref[pl.ds(at, SUB), :] = ref[m * share + r]
-            heat = ref[count * share]
-            for q in range(own_levels):
-                heat_ref[q, place ^ k] = heat if q == 0 else pltpu.roll(heat, SUB - q * share, 0)
-
-    per_tile = SUB // share
-    for m in range(count):
-        for lev in range(SUB):
-            start = b * (SUB * SUB) + (m * span * SUB + lev)
-            out_ref[m, lev] = cells_ref[pl.ds(start, SUB, stride=SUB), :]
-    for q in range(own_levels):
-        heat = heat_ref[q, b * per_tile]
-        for n in range(1, per_tile):
-            part = pltpu.roll(heat_ref[q, b * per_tile + n], n * share, 0)
-            heat = jnp.where(level // share == n, part, heat)
-        temp_ref[q] = thermal_ref[q] + WARMING_WEIGHT * heat
-
-
-def finish(place, thermal, blocks, shape, firsts, span, before):
-    shards = len(blocks)
-    count, levels, _, cols = shape
+                for q in range(own_levels):
+                    heat = ref[count * share + q]
+                    at = pl.multiple_of(((count + q) * rows + row) * SUB, SUB)
+                    cells_ref[pl.ds(at, SUB), :] = jnp.broadcast_to(heat[r : r + 1, :], (SUB, LANES))
+    for b in range(0, rows, SUB):
+        for m in range(count):
+            for lev in range(SUB):
+                start = (m * rows + b) * SUB + lev
+                out_ref[m, lev, b : b + SUB, :] = cells_ref[pl.ds(start, SUB, stride=SUB), :]
+        for q in range(own_levels):
+            heat = cells_ref[pl.ds(((count + q) * rows + b) * SUB, SUB, stride=SUB), :]
+            temp_ref[q, b : b + SUB, :] = thermal_ref[q, b : b + SUB, :] + WARMING_WEIGHT * heat
+
+
+def finish(place, thermal, blocks, shape, bands):
+    count, _, rows, _ = shape
     own_levels = thermal.shape[0]
-    assert span % SUB == 0 and len(firsts) <= 2 and all(first % SUB == 0 for first in firsts)
-    per = span // SUB
-    step = per if len(firsts) == 1 else (firsts[1] - firsts[0]) // SUB
-    assert len(firsts) == 1 or per == 1
-    row_tile = lambda i: firsts[0] // SUB + (i if len(firsts) == 1 else i * step)
+    shards = SUB // own_levels
     vmem = pl.BlockSpec(memory_space=pltpu.VMEM)
-    hold = pl.BlockSpec(memory_space=pl.ANY)
-    of_band = lambda *lead: pl.BlockSpec(
-        lead + (SUB, cols), lambda i: (0,) * len(lead) + (row_tile(i), 0)
-    )
-    total = span * len(firsts)
     return pl.pallas_call(
-        functools.partial(finish_kernel, shards=shards, span=total),
-        grid=(total // SUB,),
-        in_specs=[pl.BlockSpec(memory_space=pltpu.SMEM), of_band(own_levels)]
-        + [vmem] * shards
-        + [hold] * len(before),
-        out_specs=(of_band(count, levels), of_band(own_levels)),
+        functools.partial(finish_kernel, bands=bands, shards=shards),
+        in_specs=[pl.BlockSpec(memory_space=pltpu.SMEM)] + [vmem] * (1 + len(blocks)),
         out_shape=(jax.ShapeDtypeStruct(shape, F32), jax.ShapeDtypeStruct(thermal.shape, F32)),
-        input_output_aliases={2 + shards + i: i for i in range(len(before))},
-        scratch_shapes=[
-            pltpu.VMEM((count * total * SUB, LANES), F32),
-            pltpu.VMEM((own_levels, shards, SUB, LANES), F32),
-        ],
+        scratch_shapes=[pltpu.VMEM(((count + own_levels) * rows * SUB, LANES), F32)],
         compiler_params=grant(12),
         name="finish",
-    )(place, thermal, *blocks, *before)
+    )(place, thermal, *blocks)
 
 
 def level_sum(x):
@@ -781,14 +755,17 @@
     cleft_in, cright_in = both_sides(corner)
     inner = (flow, fstrip, left_in, right_in)
     outer = (up_in, down_in, cleft_in, cright_in)
-    quarter = rows // 4
-    bands = (((quarter,), 2 * quarter, inner), ((0, 3 * quarter), quarter, inner + outer))
+    bands = (
+        ((HALO,), rows - 2 * HALO, 1, inner),
+        ((0, rows - HALO), HALO, 2, inner + outer),
+    )
+    assert all(len(firsts) * span % shards == 0 for firsts, span, *_ in bands)
     blocks = []
-    for firsts, span, parts in bands:
-        moved = transport(place, shards, x, strip, parts, firsts, span)
+    for firsts, span, together, parts in bands:
+        moved = transport(place, shards, x, strip, parts, firsts, span, together)
         blocks.append(exchanged(moved))
     back = []
-    for n, (firsts, span, _) in enumerate(bands):
+    for n, (firsts, *_) in enumerate(bands):
         reacted = react(
             place,
             species_interaction_table,
@@ -804,12 +781,13 @@
     east_out, north_out, height_out = momentum(
         late, coriolis, inside, inner + outer, rows, own_levels
     )
-    done = ()
-    for n, (firsts, span, _) in enumerate(bands):
-        done = finish(
-            place, thermal_anomaly, back[n], species_concentrations.shape, firsts, span, done
-        )
-    updated, temperature = done
+    updated, temperature = finish(
+        place,
+        thermal_anomaly,
+        back[0] + back[1],
+        species_concentrations.shape,
+        tuple((firsts, span) for firsts, span, *_ in bands),
+    )
     vel = (own_levels, rows, cols)
     return (
         updated,

time: 89.2 us -> 98.4 us (1.10)
  waiting for transfers between devices: 28.9 us -> 40.6 us
  starting transfers between devices: 32.1 us -> 29.6 us
    ppermute x15, waiting for transfers between devices: 25.9 us -> 36.6 us  [to_peer(): return lax.ppermute(block, 'trc', [(i, i ^ k) for i in range(count)])]
    ppermute x15, starting transfers between devices: 25.8 us -> 23.5 us  [to_peer(): return lax.ppermute(block, 'trc', [(i, i ^ k) for i in range(count)])]
    ppermute x2, waiting for transfers between devices: 0.01 us -> 1.75 us  [from_lat(): lax.ppermute(block, 'lat', [(i, i + step) for i in range(count) if 0 <= i...]
  transfers between devices with their start and end apart: 19 -> 19, of which waited for: 7 -> 5; matrix products, arithmetic and copies ran while one was open for 0% -> 0% of each run, Pallas kernels for 27% -> 19%
where the time goes in v1:
time: 98.4 us; the launch traced here: 98.1 us
  waiting for transfers between devices  40.6 us (41%)
  starting transfers between devices  29.6 us (30%)
  Pallas kernels  24.9 us (25%)
  local copies, waits for them, and re-layouts  1.26 us (1%)
    ppermute x15, waiting for transfers between devices, to_peer(): return lax.ppermute(block, 'trc', [(i, i ^ k) for i in range(count)])  36.6 us
    ppermute x15, starting transfers between devices, to_peer(): return lax.ppermute(block, 'trc', [(i, i ^ k) for i in range(count)])  23.5 us
    pallas_call x2, Pallas kernels, transport(): pl.pallas_call(functools.partial(transport_kernel, firsts=firsts, span=sp...  12.4 us
    pallas_call x2, Pallas kernels, react(): pl.pallas_call(functools.partial(react_kernel, firsts=firsts), in_specs=[...  5.46 us
    pallas_call x1, Pallas kernels, momentum(): pl.pallas_call(momentum_kernel, in_specs=[pl.BlockSpec(memory_space=pltpu...  4.04 us
    ppermute x2, starting transfers between devices, both_sides(): lax.ppermute(block, 'lon', [(i, (i + 1) % count) for i in range(count)])  3.28 us
    ppermute x2, starting transfers between devices, from_lat(): lax.ppermute(block, 'lat', [(i, i + step) for i in range(count) if 0 <= i...  2.87 us
    ppermute x2, waiting for transfers between devices, both_sides(): lax.ppermute(block, 'lon', [(i, (i + 1) % count) for i in range(count)])  2.31 us
  transfers between devices with their start and end apart: 19, of which 5 were waited for; matrix products, arithmetic and copies ran while one was open for 0% of the time, Pallas kernels for 19%

profile of v1, /device:TPU:0, one launch (start us, length us, event | category | flops | bytes accessed | tf_op | source)
XLA Modules:
  0.0 98.1 jit_solution(16439260153969051309)
XLA Ops:
  0.7 0.8 pad_maximum_fusion.own_ref
  1.4 5.1 %collective-permute-start.2 = (f32[2,64,128]{2,1,0:T(8,128)S(1)}, f32[2,64,128]{2,1,0:T(8,128)S(1)}, u32[]{:S(2)}, u32[]{:S(2)}) collective-permute-start(f32[2,64,128]{2,1,0:T(8,128)S(1)} %pad_maximum_fusion.own_ref), channel_id=1, source_target_pairs={{0,24},{8,16},{16,8},{24,0},{1,25},{9,17},{17,9},{25,1},{2,26},{10... | collective-permute-start | bytes 196616 | tf_op jit(solution)/shard_map/ppermute | solution.py:693
  6.5 0.6 collective-permute-start
  7.2 1.2 %copy-done = f32[8,8,32,128]{3,2,1,0:T(8,128)S(1)} copy-done((f32[8,8,32,128]{3,2,1,0:T(8,128)S(1)}, f32[8,8,32,128]{3,2,1,0:T(8,128)}, u32[]{:S(2)}) %copy-start) | copy-done | bytes 1048600
  8.4 1.1 %pack_tracers.1 = (f32[32,8,128]{2,1,0:T(8,128)S(1)}, f32[32,8,128]{2,1,0:T(8,128)S(1)}, f32[32,8,128]{2,1,0:T(8,128)S(1)}, f32[16,8,128]{2,1,0:T(8,128)S(1)}) custom-call(f32[8,256,128]{2,1,0:T(8,128)S(1)} %bitcast.6), custom_call_target="tpu_custom_call" | custom-call | tf_op jit(solution)/shard_map/pack_tracers/pallas_call | solution.py:115
  9.5 2.7 %collective-permute-done.1.refs_1_ = f32[2,64,128]{2,1,0:T(8,128)S(1)} collective-permute-done((f32[2,64,128]{2,1,0:T(8,128)S(1)}, f32[2,64,128]{2,1,0:T(8,128)S(1)}, u32[]{:S(2)}, u32[]{:S(2)}) %collective-permute-start.1) | collective-permute-done | bytes 65568 | tf_op jit(solution)/shard_map/ppermute | solution.py:693
  12.1 0.4 pack_flow.1
  12.5 1.6 %collective-permute-start.10 = (f32[44,8,128]{2,1,0:T(8,128)S(1)}, f32[44,8,128]{2,1,0:T(8,128)S(1)}, u32[]{:S(2)}, u32[]{:S(2)}) collective-permute-start(f32[44,8,128]{2,1,0:T(8,128)S(1)} %get-tuple-element.52), channel_id=1, source_target_pairs={{0,2},{2,4},{4,6},{1,3},{3,5},{5,7},{8,10},{10,12},{12,14},{9,11},... | collective-permute-start | bytes 540680 | tf_op jit(solution)/shard_map/ppermute | solution.py:705
  14.1 1.3 %collective-permute-start.11 = (f32[44,8,128]{2,1,0:T(8,128)S(1)}, f32[44,8,128]{2,1,0:T(8,128)S(1)}, u32[]{:S(2)}, u32[]{:S(2)}) collective-permute-start(f32[44,8,128]{2,1,0:T(8,128)S(1)} %get-tuple-element.53), channel_id=1, source_target_pairs={{2,0},{4,2},{6,4},{3,1},{5,3},{7,5},{10,8},{12,10},{14,12},{11,9},... | collective-permute-start | bytes 540680 | tf_op jit(solution)/shard_map/ppermute | solution.py:705
  15.4 1.7 %collective-permute-start.3 = (f32[24,8,128]{2,1,0:T(8,128)S(1)}, f32[24,8,128]{2,1,0:T(8,128)S(1)}, u32[]{:S(2)}, u32[]{:S(2)}) collective-permute-start(f32[24,8,128]{2,1,0:T(8,128)S(1)} %get-tuple-element.43), channel_id=1, source_target_pairs={{0,1},{1,0},{2,3},{3,2},{4,5},{5,4},{6,7},{7,6},{8,9},{9,8},{10,11... | collective-permute-start | bytes 294920 | tf_op jit(solution)/shard_map/ppermute | solution.py:712
  17.1 1.7 %collective-permute-done.11.down_ref.refs_1_ = f32[44,8,128]{2,1,0:T(8,128)S(1)} collective-permute-done((f32[44,8,128]{2,1,0:T(8,128)S(1)}, f32[44,8,128]{2,1,0:T(8,128)S(1)}, u32[]{:S(2)}, u32[]{:S(2)}) %collective-permute-start.11) | collective-permute-done | bytes 180256 | tf_op jit(solution)/shard_map/ppermute | solution.py:705
  19.1 1.6 %collective-permute-start.12 = (f32[6,8,128]{2,1,0:T(8,128)S(1)}, f32[6,8,128]{2,1,0:T(8,128)S(1)}, u32[]{:S(2)}, u32[]{:S(2)}) collective-permute-start(f32[6,8,128]{2,1,0:T(8,128)S(1)} %pack_edges.1), channel_id=1, source_target_pairs={{0,1},{1,0},{2,3},{3,2},{4,5},{5,4},{6,7},{7,6},{8,9},{9,8},{10,11... | collective-permute-start | bytes 73736 | tf_op jit(solution)/shard_map/ppermute | solution.py:712
  20.7 2.3 %collective-permute-done.12.refs_2_.refs_3_.cleft_ref.cright_ref = f32[6,8,128]{2,1,0:T(8,128)S(1)} collective-permute-done((f32[6,8,128]{2,1,0:T(8,128)S(1)}, f32[6,8,128]{2,1,0:T(8,128)S(1)}, u32[]{:S(2)}, u32[]{:S(2)}) %collective-permute-start.12) | collective-permute-done | bytes 24608 | tf_op jit(solution)/shard_map/ppermute | solution.py:712
  23.0 4.4 %transport.3 = (f32[16,8,128]{2,1,0:T(8,128)S(1)}, f32[16,8,128]{2,1,0:T(8,128)S(1)}, f32[16,8,128]{2,1,0:T(8,128)S(1)}, f32[16,8,128]{2,1,0:T(8,128)S(1)}) custom-call(s32[1]{0:T(128)} %bitcast.place_ref, f32[8,256,128]{2,1,0:T(8,128)S(1)} %bitcast.7, f32[32,8,128]{2,1,0:T(8,128)S(1)} %get-tuple-element.37.strip_ref, ...), custom_call_target="tpu_custom_call" | custom-call | tf_op jit(solution)/shard_map/transport/pallas_call | solution.py:416
  27.3 1.1 %collective-permute-start.13 = (f32[16,8,128]{2,1,0:T(8,128)S(1)}, f32[16,8,128]{2,1,0:T(8,128)S(1)}, u32[]{:S(2)}, u32[]{:S(2)}) collective-permute-start(f32[16,8,128]{2,1,0:T(8,128)S(1)} %get-tuple-element.55), channel_id=1, source_target_pairs={{0,8},{8,0},{16,24},{24,16},{1,9},{9,1},{17,25},{25,17},{2,10},{10... | collective-permute-start | bytes 196616 | tf_op jit(solution)/shard_map/ppermute | solution.py:693
  28.5 8.1 %transport.2 = (f32[48,8,128]{2,1,0:T(8,128)S(1)}, f32[48,8,128]{2,1,0:T(8,128)S(1)}, f32[48,8,128]{2,1,0:T(8,128)S(1)}, f32[48,8,128]{2,1,0:T(8,128)S(1)}) custom-call(s32[1]{0:T(128)} %bitcast.place_ref, f32[8,256,128]{2,1,0:T(8,128)S(1)} %bitcast.8, f32[32,8,128]{2,1,0:T(8,128)S(1)} %get-tuple-element.37.strip_ref, ...), custom_call_target="tpu_custom_call" | custom-call | tf_op jit(solution)/shard_map/transport/pallas_call | solution.py:416
  36.6 1.0 %collective-permute-start.4 = (f32[48,8,128]{2,1,0:T(8,128)S(1)}, f32[48,8,128]{2,1,0:T(8,128)S(1)}, u32[]{:S(2)}, u32[]{:S(2)}) collective-permute-start(f32[48,8,128]{2,1,0:T(8,128)S(1)} %get-tuple-element.45), channel_id=1, source_target_pairs={{0,8},{8,0},{16,24},{24,16},{1,9},{9,1},{17,25},{25,17},{2,10},{10... | collective-permute-start | bytes 589832 | tf_op jit(solution)/shard_map/ppermute | solution.py:693
  37.6 1.6 %collective-permute-start.5 = (f32[48,8,128]{2,1,0:T(8,128)S(1)}, f32[48,8,128]{2,1,0:T(8,128)S(1)}, u32[]{:S(2)}, u32[]{:S(2)}) collective-permute-start(f32[48,8,128]{2,1,0:T(8,128)S(1)} %get-tuple-element.46), channel_id=1, source_target_pairs={{0,16},{8,24},{16,0},{24,8},{1,17},{9,25},{17,1},{25,9},{2,18},{10... | collective-permute-start | bytes 589832 | tf_op jit(solution)/shard_map/ppermute | solution.py:693
  39.2 1.9 %collective-permute-start.6 = (f32[48,8,128]{2,1,0:T(8,128)S(1)}, f32[48,8,128]{2,1,0:T(8,128)S(1)}, u32[]{:S(2)}, u32[]{:S(2)}) collective-permute-start(f32[48,8,128]{2,1,0:T(8,128)S(1)} %get-tuple-element.47), channel_id=1, source_target_pairs={{0,24},{8,16},{16,8},{24,0},{1,25},{9,17},{17,9},{25,1},{2,26},{10... | collective-permute-start | bytes 589832 | tf_op jit(solution)/shard_map/ppermute | solution.py:693
  41.0 1.3 %collective-permute-start.14 = (f32[16,8,128]{2,1,0:T(8,128)S(1)}, f32[16,8,128]{2,1,0:T(8,128)S(1)}, u32[]{:S(2)}, u32[]{:S(2)}) collective-permute-start(f32[16,8,128]{2,1,0:T(8,128)S(1)} %get-tuple-element.56), channel_id=1, source_target_pairs={{0,16},{8,24},{16,0},{24,8},{1,17},{9,25},{17,1},{25,9},{2,18},{10... | collective-permute-start | bytes 196616 | tf_op jit(solution)/shard_map/ppermute | solution.py:693
  42.3 1.1 %collective-permute-start.15 = (f32[16,8,128]{2,1,0:T(8,128)S(1)}, f32[16,8,128]{2,1,0:T(8,128)S(1)}, u32[]{:S(2)}, u32[]{:S(2)}) collective-permute-start(f32[16,8,128]{2,1,0:T(8,128)S(1)} %get-tuple-element.57), channel_id=1, source_target_pairs={{0,24},{8,16},{16,8},{24,0},{1,25},{9,17},{17,9},{25,1},{2,26},{10... | collective-permute-start | bytes 196616 | tf_op jit(solution)/shard_map/ppermute | solution.py:693
  43.6 18.1 %collective-permute-done.14.refs_2_ = f32[16,8,128]{2,1,0:T(8,128)S(1)} collective-permute-done((f32[16,8,128]{2,1,0:T(8,128)S(1)}, f32[16,8,128]{2,1,0:T(8,128)S(1)}, u32[]{:S(2)}, u32[]{:S(2)}) %collective-permute-start.14) | collective-permute-done | bytes 65568 | tf_op jit(solution)/shard_map/ppermute | solution.py:693
  61.7 2.6 %react.3 = (f32[18,8,128]{2,1,0:T(8,128)S(1)}, f32[18,8,128]{2,1,0:T(8,128)S(1)}, f32[18,8,128]{2,1,0:T(8,128)S(1)}, f32[18,8,128]{2,1,0:T(8,128)S(1)}) custom-call(s32[1]{0:T(128)} %bitcast.place_ref, f32[32,32]{1,0:T(8,128)S(1)} %copy-done.3, f32[32]{0:T(128)S(1)} %copy-done.6, f32[32]{0:T(128)S(1)} %copy-done.7, f32[32]{0:T(128)S(1)} %cosine_add_fusion.surface_ref, ...), custom_call_target="tpu_custom_call" | custom-call | tf_op jit(solution)/shard_map/react/pallas_call | solution.py:505
  64.2 2.0 %collective-permute-start.16 = (f32[18,8,128]{2,1,0:T(8,128)S(1)}, f32[18,8,128]{2,1,0:T(8,128)S(1)}, u32[]{:S(2)}, u32[]{:S(2)}) collective-permute-start(f32[18,8,128]{2,1,0:T(8,128)S(1)} %get-tuple-element.60), channel_id=1, source_target_pairs={{0,8},{8,0},{16,24},{24,16},{1,9},{9,1},{17,25},{25,17},{2,10},{10... | collective-permute-start | bytes 221192 | tf_op jit(solution)/shard_map/ppermute | solution.py:693
  66.3 2.9 %react.2 = (f32[50,8,128]{2,1,0:T(8,128)S(1)}, f32[50,8,128]{2,1,0:T(8,128)S(1)}, f32[50,8,128]{2,1,0:T(8,128)S(1)}, f32[50,8,128]{2,1,0:T(8,128)S(1)}) custom-call(s32[1]{0:T(128)} %bitcast.place_ref, f32[32,32]{1,0:T(8,128)S(1)} %copy-done.3, f32[32]{0:T(128)S(1)} %copy-done.6, f32[32]{0:T(128)S(1)} %copy-done.7, f32[32]{0:T(128)S(1)} %cosine_add_fusion.surface_ref, ...), custom_call_target="tpu_custom_call" | custom-call | tf_op jit(solution)/shard_map/react/pallas_call | solution.py:505
  69.3 3.6 %collective-permute-start.8 = (f32[50,8,128]{2,1,0:T(8,128)S(1)}, f32[50,8,128]{2,1,0:T(8,128)S(1)}, u32[]{:S(2)}, u32[]{:S(2)}) collective-permute-start(f32[50,8,128]{2,1,0:T(8,128)S(1)} %get-tuple-element.50), channel_id=1, source_target_pairs={{0,16},{8,24},{16,0},{24,8},{1,17},{9,25},{17,1},{25,9},{2,18},{10... | collective-permute-start | bytes 614408 | tf_op jit(solution)/shard_map/ppermute | solution.py:693
  72.9 0.7 collective-permute-start.9
  73.7 0.9 collective-permute-start.17
  74.6 2.4 %collective-permute-start.18 = (f32[18,8,128]{2,1,0:T(8,128)S(1)}, f32[18,8,128]{2,1,0:T(8,128)S(1)}, u32[]{:S(2)}, u32[]{:S(2)}) collective-permute-start(f32[18,8,128]{2,1,0:T(8,128)S(1)} %get-tuple-element.62), channel_id=1, source_target_pairs={{0,24},{8,16},{16,8},{24,0},{1,25},{9,17},{17,9},{25,1},{2,26},{10... | collective-permute-start | bytes 221192 | tf_op jit(solution)/shard_map/ppermute | solution.py:693
  77.0 4.0 %momentum.1 = (f32[64,128]{1,0:T(8,128)}, f32[64,128]{1,0:T(8,128)}, f32[32,128]{1,0:T(8,128)}) custom-call(s32[1]{0:T(128)} %bitcast.place_ref, f32[36]{0:T(128)S(1)} %sine_multiply_fusion.coriolis_ref, f32[36]{0:T(128)S(1)} %and_convert_fusion.inside_ref, f32[96,8,128]{2,1,0:T(8,128)S(1)} %get-tuple-element.41.flow_ref, ...), custom_call_target="tpu_custom_call" | custom-call | tf_op jit(solution)/shard_map/momentum/pallas_call | solution.py:673
  81.0 15.8 %collective-permute-done.17.refs_6_ = f32[18,8,128]{2,1,0:T(8,128)S(1)} collective-permute-done((f32[18,8,128]{2,1,0:T(8,128)S(1)}, f32[18,8,128]{2,1,0:T(8,128)S(1)}, u32[]{:S(2)}, u32[]{:S(2)}) %collective-permute-start.17) | collective-permute-done | bytes 73760 | tf_op jit(solution)/shard_map/ppermute | solution.py:693
  96.8 1.3 %finish.1 = (f32[8,8,32,128]{3,2,1,0:T(8,128)}, f32[2,32,128]{2,1,0:T(8,128)}) custom-call(s32[1]{0:T(128)} %bitcast.place_ref, f32[2,32,128]{2,1,0:T(8,128)S(1)} %copy-done.4, f32[50,8,128]{2,1,0:T(8,128)S(1)} %get-tuple-element.48.refs_0_, f32[50,8,128]{2,1,0:T(8,128)S(1)} %collective-permute-done.7.refs_1_, ...), custom_call_target="tpu_custom_call" | custom-call | tf_op jit(solution)/shard_map/finish/pallas_call | solution.py:553
  (36 shorter events, 0.6 us)
Async XLA Ops:
  0.6 11.5 %copy-start.2 = (s32[32,128]{1,0:T(8,128)S(1)}, s32[32,128]{1,0:T(8,128)}, u32[]{:S(2)}) copy-start(s32[32,128]{1,0:T(8,128)} %tally_ref.3) | copy-start | bytes 49156
  0.6 11.5 %copy-start.5 = (f32[32,128]{1,0:T(8,128)S(1)}, f32[32,128]{1,0:T(8,128)}, u32[]{:S(2)}) copy-start(f32[32,128]{1,0:T(8,128)} %refs_4_.1) | copy-start | bytes 49156
  1.4 8.0 %collective-permute-start.2 = (f32[2,64,128]{2,1,0:T(8,128)S(1)}, f32[2,64,128]{2,1,0:T(8,128)S(1)}, u32[]{:S(2)}, u32[]{:S(2)}) collective-permute-start(f32[2,64,128]{2,1,0:T(8,128)S(1)} %pad_maximum_fusion.own_ref), channel_id=1, source_target_pairs={{0,24},{8,16},{16,8},{24,0},{1,25},{9,17},{17,9},{25,1},{2,26},{10... | collective-permute-start | bytes 196616 | tf_op jit(solution)/shard_map/ppermute | solution.py:693
  6.5 5.6 %collective-permute-start.1 = (f32[2,64,128]{2,1,0:T(8,128)S(1)}, f32[2,64,128]{2,1,0:T(8,128)S(1)}, u32[]{:S(2)}, u32[]{:S(2)}) collective-permute-start(f32[2,64,128]{2,1,0:T(8,128)S(1)} %pad_maximum_fusion.own_ref), channel_id=1, source_target_pairs={{0,16},{8,24},{16,0},{24,8},{1,17},{9,25},{17,1},{25,9},{2,18},{10... | collective-permute-start | bytes 196616 | tf_op jit(solution)/shard_map/ppermute | solution.py:693
  6.5 5.6 %collective-permute-start = (f32[2,64,128]{2,1,0:T(8,128)S(1)}, f32[2,64,128]{2,1,0:T(8,128)S(1)}, u32[]{:S(2)}, u32[]{:S(2)}) collective-permute-start(f32[2,64,128]{2,1,0:T(8,128)S(1)} %pad_maximum_fusion.own_ref), channel_id=1, source_target_pairs={{0,8},{8,0},{16,24},{24,16},{1,9},{9,1},{17,25},{25,17},{2,10},{10... | collective-permute-start | bytes 196616 | tf_op jit(solution)/shard_map/ppermute | solution.py:693
  7.2 1.2 %copy-start = (f32[8,8,32,128]{3,2,1,0:T(8,128)S(1)}, f32[8,8,32,128]{3,2,1,0:T(8,128)}, u32[]{:S(2)}) copy-start(f32[8,8,32,128]{3,2,1,0:T(8,128)} %param.9) | copy-start | bytes 3145732
  8.4 14.6 %copy-start.1 = (f32[8,8,32,128]{3,2,1,0:T(8,128)S(1)}, f32[8,8,32,128]{3,2,1,0:T(8,128)}, u32[]{:S(2)}) copy-start(f32[8,8,32,128]{3,2,1,0:T(8,128)} %param.9) | copy-start | bytes 3145732
  12.5 4.6 %collective-permute-start.10 = (f32[44,8,128]{2,1,0:T(8,128)S(1)}, f32[44,8,128]{2,1,0:T(8,128)S(1)}, u32[]{:S(2)}, u32[]{:S(2)}) collective-permute-start(f32[44,8,128]{2,1,0:T(8,128)S(1)} %get-tuple-element.52), channel_id=1, source_target_pairs={{0,2},{2,4},{4,6},{1,3},{3,5},{5,7},{8,10},{10,12},{12,14},{9,11},... | collective-permute-start | bytes 540680 | tf_op jit(solution)/shard_map/ppermute | solution.py:705
  14.1 4.7 %collective-permute-start.11 = (f32[44,8,128]{2,1,0:T(8,128)S(1)}, f32[44,8,128]{2,1,0:T(8,128)S(1)}, u32[]{:S(2)}, u32[]{:S(2)}) collective-permute-start(f32[44,8,128]{2,1,0:T(8,128)S(1)} %get-tuple-element.53), channel_id=1, source_target_pairs={{2,0},{4,2},{6,4},{3,1},{5,3},{7,5},{10,8},{12,10},{14,12},{11,9},... | collective-permute-start | bytes 540680 | tf_op jit(solution)/shard_map/ppermute | solution.py:705
  15.4 5.2 %collective-permute-start.3 = (f32[24,8,128]{2,1,0:T(8,128)S(1)}, f32[24,8,128]{2,1,0:T(8,128)S(1)}, u32[]{:S(2)}, u32[]{:S(2)}) collective-permute-start(f32[24,8,128]{2,1,0:T(8,128)S(1)} %get-tuple-element.43), channel_id=1, source_target_pairs={{0,1},{1,0},{2,3},{3,2},{4,5},{5,4},{6,7},{7,6},{8,9},{9,8},{10,11... | collective-permute-start | bytes 294920 | tf_op jit(solution)/shard_map/ppermute | solution.py:712
  19.1 3.9 %collective-permute-start.12 = (f32[6,8,128]{2,1,0:T(8,128)S(1)}, f32[6,8,128]{2,1,0:T(8,128)S(1)}, u32[]{:S(2)}, u32[]{:S(2)}) collective-permute-start(f32[6,8,128]{2,1,0:T(8,128)S(1)} %pack_edges.1), channel_id=1, source_target_pairs={{0,1},{1,0},{2,3},{3,2},{4,5},{5,4},{6,7},{7,6},{8,9},{9,8},{10,11... | collective-permute-start | bytes 73736 | tf_op jit(solution)/shard_map/ppermute | solution.py:712
  27.3 15.0 %collective-permute-start.13 = (f32[16,8,128]{2,1,0:T(8,128)S(1)}, f32[16,8,128]{2,1,0:T(8,128)S(1)}, u32[]{:S(2)}, u32[]{:S(2)}) collective-permute-start(f32[16,8,128]{2,1,0:T(8,128)S(1)} %get-tuple-element.55), channel_id=1, source_target_pairs={{0,8},{8,0},{16,24},{24,16},{1,9},{9,1},{17,25},{25,17},{2,10},{10... | collective-permute-start | bytes 196616 | tf_op jit(solution)/shard_map/ppermute | solution.py:693
  28.5 33.2 %copy-start.3 = (f32[32,32]{1,0:T(8,128)S(1)}, f32[32,32]{1,0:T(8,128)}, u32[]{:S(2)}) copy-start(f32[32,32]{1,0:T(8,128)} %table_ref.3) | copy-start | bytes 12292
  36.6 29.7 %collective-permute-start.4 = (f32[48,8,128]{2,1,0:T(8,128)S(1)}, f32[48,8,128]{2,1,0:T(8,128)S(1)}, u32[]{:S(2)}, u32[]{:S(2)}) collective-permute-start(f32[48,8,128]{2,1,0:T(8,128)S(1)} %get-tuple-element.45), channel_id=1, source_target_pairs={{0,8},{8,0},{16,24},{24,16},{1,9},{9,1},{17,25},{25,17},{2,10},{10... | collective-permute-start | bytes 589832 | tf_op jit(solution)/shard_map/ppermute | solution.py:693
  37.6 28.7 %collective-permute-start.5 = (f32[48,8,128]{2,1,0:T(8,128)S(1)}, f32[48,8,128]{2,1,0:T(8,128)S(1)}, u32[]{:S(2)}, u32[]{:S(2)}) collective-permute-start(f32[48,8,128]{2,1,0:T(8,128)S(1)} %get-tuple-element.46), channel_id=1, source_target_pairs={{0,16},{8,24},{16,0},{24,8},{1,17},{9,25},{17,1},{25,9},{2,18},{10... | collective-permute-start | bytes 589832 | tf_op jit(solution)/shard_map/ppermute | solution.py:693
  39.2 27.1 %collective-permute-start.6 = (f32[48,8,128]{2,1,0:T(8,128)S(1)}, f32[48,8,128]{2,1,0:T(8,128)S(1)}, u32[]{:S(2)}, u32[]{:S(2)}) collective-permute-start(f32[48,8,128]{2,1,0:T(8,128)S(1)} %get-tuple-element.47), channel_id=1, source_target_pairs={{0,24},{8,16},{16,8},{24,0},{1,25},{9,17},{17,9},{25,1},{2,26},{10... | collective-permute-start | bytes 589832 | tf_op jit(solution)/shard_map/ppermute | solution.py:693
  41.0 20.6 %collective-permute-start.14 = (f32[16,8,128]{2,1,0:T(8,128)S(1)}, f32[16,8,128]{2,1,0:T(8,128)S(1)}, u32[]{:S(2)}, u32[]{:S(2)}) collective-permute-start(f32[16,8,128]{2,1,0:T(8,128)S(1)} %get-tuple-element.56), channel_id=1, source_target_pairs={{0,16},{8,24},{16,0},{24,8},{1,17},{9,25},{17,1},{25,9},{2,18},{10... | collective-permute-start | bytes 196616 | tf_op jit(solution)/shard_map/ppermute | solution.py:693
  42.3 19.3 %collective-permute-start.15 = (f32[16,8,128]{2,1,0:T(8,128)S(1)}, f32[16,8,128]{2,1,0:T(8,128)S(1)}, u32[]{:S(2)}, u32[]{:S(2)}) collective-permute-start(f32[16,8,128]{2,1,0:T(8,128)S(1)} %get-tuple-element.57), channel_id=1, source_target_pairs={{0,24},{8,16},{16,8},{24,0},{1,25},{9,17},{17,9},{25,1},{2,26},{10... | collective-permute-start | bytes 196616 | tf_op jit(solution)/shard_map/ppermute | solution.py:693
  43.5 18.1 %copy-start.6 = (f32[32]{0:T(128)S(1)}, f32[32]{0:T(128)}, u32[]{:S(2)}) copy-start(f32[32]{0:T(128)} %pace_ref.3) | copy-start | bytes 388
  43.5 18.1 %copy-start.7 = (f32[32]{0:T(128)S(1)}, f32[32]{0:T(128)}, u32[]{:S(2)}) copy-start(f32[32]{0:T(128)} %uptake_ref.3) | copy-start | bytes 388
  64.2 10.3 %collective-permute-start.16 = (f32[18,8,128]{2,1,0:T(8,128)S(1)}, f32[18,8,128]{2,1,0:T(8,128)S(1)}, u32[]{:S(2)}, u32[]{:S(2)}) collective-permute-start(f32[18,8,128]{2,1,0:T(8,128)S(1)} %get-tuple-element.60), channel_id=1, source_target_pairs={{0,8},{8,0},{16,24},{24,16},{1,9},{9,1},{17,25},{25,17},{2,10},{10... | collective-permute-start | bytes 221192 | tf_op jit(solution)/shard_map/ppermute | solution.py:693
  69.2 27.6 %collective-permute-start.7 = (f32[50,8,128]{2,1,0:T(8,128)S(1)}, f32[50,8,128]{2,1,0:T(8,128)S(1)}, u32[]{:S(2)}, u32[]{:S(2)}) collective-permute-start(f32[50,8,128]{2,1,0:T(8,128)S(1)} %get-tuple-element.49), channel_id=1, source_target_pairs={{0,8},{8,0},{16,24},{24,16},{1,9},{9,1},{17,25},{25,17},{2,10},{10... | collective-permute-start | bytes 614408 | tf_op jit(solution)/shard_map/ppermute | solution.py:693
  69.3 27.5 %collective-permute-start.8 = (f32[50,8,128]{2,1,0:T(8,128)S(1)}, f32[50,8,128]{2,1,0:T(8,128)S(1)}, u32[]{:S(2)}, u32[]{:S(2)}) collective-permute-start(f32[50,8,128]{2,1,0:T(8,128)S(1)} %get-tuple-element.50), channel_id=1, source_target_pairs={{0,16},{8,24},{16,0},{24,8},{1,17},{9,25},{17,1},{25,9},{2,18},{10... | collective-permute-start | bytes 614408 | tf_op jit(solution)/shard_map/ppermute | solution.py:693
  72.9 23.9 %collective-permute-start.9 = (f32[50,8,128]{2,1,0:T(8,128)S(1)}, f32[50,8,128]{2,1,0:T(8,128)S(1)}, u32[]{:S(2)}, u32[]{:S(2)}) collective-permute-start(f32[50,8,128]{2,1,0:T(8,128)S(1)} %get-tuple-element.51), channel_id=1, source_target_pairs={{0,24},{8,16},{16,8},{24,0},{1,25},{9,17},{17,9},{25,1},{2,26},{10... | collective-permute-start | bytes 614408 | tf_op jit(solution)/shard_map/ppermute | solution.py:693
  73.7 23.1 %collective-permute-start.17 = (f32[18,8,128]{2,1,0:T(8,128)S(1)}, f32[18,8,128]{2,1,0:T(8,128)S(1)}, u32[]{:S(2)}, u32[]{:S(2)}) collective-permute-start(f32[18,8,128]{2,1,0:T(8,128)S(1)} %get-tuple-element.61), channel_id=1, source_target_pairs={{0,16},{8,24},{16,0},{24,8},{1,17},{9,25},{17,1},{25,9},{2,18},{10... | collective-permute-start | bytes 221192 | tf_op jit(solution)/shard_map/ppermute | solution.py:693
  74.6 22.2 %collective-permute-start.18 = (f32[18,8,128]{2,1,0:T(8,128)S(1)}, f32[18,8,128]{2,1,0:T(8,128)S(1)}, u32[]{:S(2)}, u32[]{:S(2)}) collective-permute-start(f32[18,8,128]{2,1,0:T(8,128)S(1)} %get-tuple-element.62), channel_id=1, source_target_pairs={{0,24},{8,16},{16,8},{24,0},{1,25},{9,17},{17,9},{25,1},{2,26},{10... | collective-permute-start | bytes 221192 | tf_op jit(solution)/shard_map/ppermute | solution.py:693
  77.0 19.9 %copy-start.4 = (f32[2,32,128]{2,1,0:T(8,128)S(1)}, f32[2,32,128]{2,1,0:T(8,128)}, u32[]{:S(2)}) copy-start(f32[2,32,128]{2,1,0:T(8,128)} %thermal_ref.1) | copy-start | bytes 98308

commit v2 on v1

--- a/solution.py
+++ b/solution.py
@@ -755,9 +755,10 @@
     cleft_in, cright_in = both_sides(corner)
     inner = (flow, fstrip, left_in, right_in)
     outer = (up_in, down_in, cleft_in, cright_in)
+    edge = HALO + 2
     bands = (
-        ((HALO,), rows - 2 * HALO, 1, inner),
-        ((0, rows - HALO), HALO, 2, inner + outer),
+        ((edge,), rows - 2 * edge, 2, inner),
+        ((0, rows - edge), edge, 2, inner + outer),
     )
     assert all(len(firsts) * span % shards == 0 for firsts, span, *_ in bands)
     blocks = []

time: 98.4 us -> 84 us (0.85)
  waiting for transfers between devices: 40.6 us -> 19.6 us
  starting transfers between devices: 29.6 us -> 36.3 us
    ppermute x15, waiting for transfers between devices: 36.6 us -> 16.6 us  [to_peer(): return lax.ppermute(block, 'trc', [(i, i ^ k) for i in range(count)])]
    ppermute x15, starting transfers between devices: 23.5 us -> 30.1 us  [to_peer(): return lax.ppermute(block, 'trc', [(i, i ^ k) for i in range(count)])]
    ppermute x2, waiting for transfers between devices: 1.75 us -> 0.01 us  [from_lat(): lax.ppermute(block, 'lat', [(i, i + step) for i in range(count) if 0 <= i...]
  transfers between devices with their start and end apart: 19 -> 19, of which waited for: 5 -> 5; matrix products, arithmetic and copies ran while one was open for 0% -> 0% of each run, Pallas kernels for 19% -> 28%
where the time goes in v2:
time: 84 us; the launch traced here: 83.8 us
  starting transfers between devices  36.3 us (43%)
  Pallas kernels  25 us (30%)
  waiting for transfers between devices  19.6 us (23%)
  local copies, waits for them, and re-layouts  1.26 us (2%)
  other arithmetic  0.97 us (1%)
    ppermute x15, starting transfers between devices, to_peer(): return lax.ppermute(block, 'trc', [(i, i ^ k) for i in range(count)])  30.1 us
    ppermute x15, waiting for transfers between devices, to_peer(): return lax.ppermute(block, 'trc', [(i, i ^ k) for i in range(count)])  16.6 us
    pallas_call x2, Pallas kernels, transport(): pl.pallas_call(functools.partial(transport_kernel, firsts=firsts, span=sp...  12.9 us
    pallas_call x2, Pallas kernels, react(): pl.pallas_call(functools.partial(react_kernel, firsts=firsts), in_specs=[...  5.06 us
    pallas_call x1, Pallas kernels, momentum(): pl.pallas_call(momentum_kernel, in_specs=[pl.BlockSpec(memory_space=pltpu...  4.04 us
    ppermute x2, starting transfers between devices, both_sides(): lax.ppermute(block, 'lon', [(i, (i + 1) % count) for i in range(count)])  3.28 us
    ppermute x2, waiting for transfers between devices, both_sides(): lax.ppermute(block, 'lon', [(i, (i + 1) % count) for i in range(count)])  2.98 us
    ppermute x2, starting transfers between devices, from_lat(): lax.ppermute(block, 'lat', [(i, i + step) for i in range(count) if 0 <= i...  2.87 us
  transfers between devices with their start and end apart: 19, of which 5 were waited for; matrix products, arithmetic and copies ran while one was open for 0% of the time, Pallas kernels for 28%

profile of v2, /device:TPU:0, one launch (start us, length us, event | category | flops | bytes accessed | tf_op | source)
XLA Modules:
  0.0 83.8 jit_solution(1545390066398029332)
XLA Ops:
  0.7 0.8 pad_maximum_fusion.own_ref
  1.4 5.1 %collective-permute-start.2 = (f32[2,64,128]{2,1,0:T(8,128)S(1)}, f32[2,64,128]{2,1,0:T(8,128)S(1)}, u32[]{:S(2)}, u32[]{:S(2)}) collective-permute-start(f32[2,64,128]{2,1,0:T(8,128)S(1)} %pad_maximum_fusion.own_ref), channel_id=1, source_target_pairs={{0,24},{8,16},{16,8},{24,0},{1,25},{9,17},{17,9},{25,1},{2,26},{10... | collective-permute-start | bytes 196616 | tf_op jit(solution)/shard_map/ppermute | solution.py:693
  6.5 0.6 collective-permute-start
  7.2 1.2 %copy-done = f32[8,8,32,128]{3,2,1,0:T(8,128)S(1)} copy-done((f32[8,8,32,128]{3,2,1,0:T(8,128)S(1)}, f32[8,8,32,128]{3,2,1,0:T(8,128)}, u32[]{:S(2)}) %copy-start) | copy-done | bytes 1048600
  8.4 1.1 %pack_tracers.1 = (f32[32,8,128]{2,1,0:T(8,128)S(1)}, f32[32,8,128]{2,1,0:T(8,128)S(1)}, f32[32,8,128]{2,1,0:T(8,128)S(1)}, f32[16,8,128]{2,1,0:T(8,128)S(1)}) custom-call(f32[8,256,128]{2,1,0:T(8,128)S(1)} %bitcast.6), custom_call_target="tpu_custom_call" | custom-call | tf_op jit(solution)/shard_map/pack_tracers/pallas_call | solution.py:115
  9.5 2.7 %collective-permute-done.1.refs_1_ = f32[2,64,128]{2,1,0:T(8,128)S(1)} collective-permute-done((f32[2,64,128]{2,1,0:T(8,128)S(1)}, f32[2,64,128]{2,1,0:T(8,128)S(1)}, u32[]{:S(2)}, u32[]{:S(2)}) %collective-permute-start.1) | collective-permute-done | bytes 65568 | tf_op jit(solution)/shard_map/ppermute | solution.py:693
  12.1 0.4 pack_flow.1
  12.5 1.6 %collective-permute-start.10 = (f32[44,8,128]{2,1,0:T(8,128)S(1)}, f32[44,8,128]{2,1,0:T(8,128)S(1)}, u32[]{:S(2)}, u32[]{:S(2)}) collective-permute-start(f32[44,8,128]{2,1,0:T(8,128)S(1)} %get-tuple-element.52), channel_id=1, source_target_pairs={{0,2},{2,4},{4,6},{1,3},{3,5},{5,7},{8,10},{10,12},{12,14},{9,11},... | collective-permute-start | bytes 540680 | tf_op jit(solution)/shard_map/ppermute | solution.py:705
  14.1 1.3 %collective-permute-start.11 = (f32[44,8,128]{2,1,0:T(8,128)S(1)}, f32[44,8,128]{2,1,0:T(8,128)S(1)}, u32[]{:S(2)}, u32[]{:S(2)}) collective-permute-start(f32[44,8,128]{2,1,0:T(8,128)S(1)} %get-tuple-element.53), channel_id=1, source_target_pairs={{2,0},{4,2},{6,4},{3,1},{5,3},{7,5},{10,8},{12,10},{14,12},{11,9},... | collective-permute-start | bytes 540680 | tf_op jit(solution)/shard_map/ppermute | solution.py:705
  15.4 1.7 %collective-permute-start.3 = (f32[24,8,128]{2,1,0:T(8,128)S(1)}, f32[24,8,128]{2,1,0:T(8,128)S(1)}, u32[]{:S(2)}, u32[]{:S(2)}) collective-permute-start(f32[24,8,128]{2,1,0:T(8,128)S(1)} %get-tuple-element.43), channel_id=1, source_target_pairs={{0,1},{1,0},{2,3},{3,2},{4,5},{5,4},{6,7},{7,6},{8,9},{9,8},{10,11... | collective-permute-start | bytes 294920 | tf_op jit(solution)/shard_map/ppermute | solution.py:712
  17.1 3.0 %collective-permute-done.3.left_ref.right_ref = f32[24,8,128]{2,1,0:T(8,128)S(1)} collective-permute-done((f32[24,8,128]{2,1,0:T(8,128)S(1)}, f32[24,8,128]{2,1,0:T(8,128)S(1)}, u32[]{:S(2)}, u32[]{:S(2)}) %collective-permute-start.3) | collective-permute-done | bytes 98336 | tf_op jit(solution)/shard_map/ppermute | solution.py:712
  20.1 7.8 %transport.2 = (f32[40,8,128]{2,1,0:T(8,128)S(1)}, f32[40,8,128]{2,1,0:T(8,128)S(1)}, f32[40,8,128]{2,1,0:T(8,128)S(1)}, f32[40,8,128]{2,1,0:T(8,128)S(1)}) custom-call(s32[1]{0:T(128)} %bitcast.place_ref, f32[8,256,128]{2,1,0:T(8,128)S(1)} %bitcast.7, f32[32,8,128]{2,1,0:T(8,128)S(1)} %get-tuple-element.37.strip_ref, ...), custom_call_target="tpu_custom_call" | custom-call | tf_op jit(solution)/shard_map/transport/pallas_call | solution.py:416
  27.9 0.9 %collective-permute-start.4 = (f32[40,8,128]{2,1,0:T(8,128)S(1)}, f32[40,8,128]{2,1,0:T(8,128)S(1)}, u32[]{:S(2)}, u32[]{:S(2)}) collective-permute-start(f32[40,8,128]{2,1,0:T(8,128)S(1)} %get-tuple-element.45), channel_id=1, source_target_pairs={{0,8},{8,0},{16,24},{24,16},{1,9},{9,1},{17,25},{25,17},{2,10},{10... | collective-permute-start | bytes 491528 | tf_op jit(solution)/shard_map/ppermute | solution.py:693
  28.9 1.6 %collective-permute-start.12 = (f32[6,8,128]{2,1,0:T(8,128)S(1)}, f32[6,8,128]{2,1,0:T(8,128)S(1)}, u32[]{:S(2)}, u32[]{:S(2)}) collective-permute-start(f32[6,8,128]{2,1,0:T(8,128)S(1)} %pack_edges.1), channel_id=1, source_target_pairs={{0,1},{1,0},{2,3},{3,2},{4,5},{5,4},{6,7},{7,6},{8,9},{9,8},{10,11... | collective-permute-start | bytes 73736 | tf_op jit(solution)/shard_map/ppermute | solution.py:712
  30.5 2.2 %collective-permute-start.5 = (f32[40,8,128]{2,1,0:T(8,128)S(1)}, f32[40,8,128]{2,1,0:T(8,128)S(1)}, u32[]{:S(2)}, u32[]{:S(2)}) collective-permute-start(f32[40,8,128]{2,1,0:T(8,128)S(1)} %get-tuple-element.46), channel_id=1, source_target_pairs={{0,16},{8,24},{16,0},{24,8},{1,17},{9,25},{17,1},{25,9},{2,18},{10... | collective-permute-start | bytes 491528 | tf_op jit(solution)/shard_map/ppermute | solution.py:693
  32.7 1.5 %collective-permute-start.6 = (f32[40,8,128]{2,1,0:T(8,128)S(1)}, f32[40,8,128]{2,1,0:T(8,128)S(1)}, u32[]{:S(2)}, u32[]{:S(2)}) collective-permute-start(f32[40,8,128]{2,1,0:T(8,128)S(1)} %get-tuple-element.47), channel_id=1, source_target_pairs={{0,24},{8,16},{16,8},{24,0},{1,25},{9,17},{17,9},{25,1},{2,26},{10... | collective-permute-start | bytes 491528 | tf_op jit(solution)/shard_map/ppermute | solution.py:693
  34.3 5.1 %transport.3 = (f32[24,8,128]{2,1,0:T(8,128)S(1)}, f32[24,8,128]{2,1,0:T(8,128)S(1)}, f32[24,8,128]{2,1,0:T(8,128)S(1)}, f32[24,8,128]{2,1,0:T(8,128)S(1)}) custom-call(s32[1]{0:T(128)} %bitcast.place_ref, f32[8,256,128]{2,1,0:T(8,128)S(1)} %bitcast.8, f32[32,8,128]{2,1,0:T(8,128)S(1)} %get-tuple-element.37.strip_ref, ...), custom_call_target="tpu_custom_call" | custom-call | tf_op jit(solution)/shard_map/transport/pallas_call | solution.py:416
  39.5 2.9 %collective-permute-start.14 = (f32[24,8,128]{2,1,0:T(8,128)S(1)}, f32[24,8,128]{2,1,0:T(8,128)S(1)}, u32[]{:S(2)}, u32[]{:S(2)}) collective-permute-start(f32[24,8,128]{2,1,0:T(8,128)S(1)} %get-tuple-element.56), channel_id=1, source_target_pairs={{0,16},{8,24},{16,0},{24,8},{1,17},{9,25},{17,1},{25,9},{2,18},{10... | collective-permute-start | bytes 294920 | tf_op jit(solution)/shard_map/ppermute | solution.py:693
  42.4 1.5 %collective-permute-start.15 = (f32[24,8,128]{2,1,0:T(8,128)S(1)}, f32[24,8,128]{2,1,0:T(8,128)S(1)}, u32[]{:S(2)}, u32[]{:S(2)}) collective-permute-start(f32[24,8,128]{2,1,0:T(8,128)S(1)} %get-tuple-element.57), channel_id=1, source_target_pairs={{0,24},{8,16},{16,8},{24,0},{1,25},{9,17},{17,9},{25,1},{2,26},{10... | collective-permute-start | bytes 294920 | tf_op jit(solution)/shard_map/ppermute | solution.py:693
  44.0 1.5 %collective-permute-done.5.refs_2_ = f32[40,8,128]{2,1,0:T(8,128)S(1)} collective-permute-done((f32[40,8,128]{2,1,0:T(8,128)S(1)}, f32[40,8,128]{2,1,0:T(8,128)S(1)}, u32[]{:S(2)}, u32[]{:S(2)}) %collective-permute-start.5) | collective-permute-done | bytes 163872 | tf_op jit(solution)/shard_map/ppermute | solution.py:693
  45.6 2.6 %react.2 = (f32[42,8,128]{2,1,0:T(8,128)S(1)}, f32[42,8,128]{2,1,0:T(8,128)S(1)}, f32[42,8,128]{2,1,0:T(8,128)S(1)}, f32[42,8,128]{2,1,0:T(8,128)S(1)}) custom-call(s32[1]{0:T(128)} %bitcast.place_ref, f32[32,32]{1,0:T(8,128)S(1)} %copy-done.3, f32[32]{0:T(128)S(1)} %copy-done.6, f32[32]{0:T(128)S(1)} %copy-done.7, f32[32]{0:T(128)S(1)} %cosine_add_fusion.surface_ref, ...), custom_call_target="tpu_custom_call" | custom-call | tf_op jit(solution)/shard_map/react/pallas_call | solution.py:505
  48.2 8.2 %collective-permute-start.7 = (f32[42,8,128]{2,1,0:T(8,128)S(1)}, f32[42,8,128]{2,1,0:T(8,128)S(1)}, u32[]{:S(2)}, u32[]{:S(2)}) collective-permute-start(f32[42,8,128]{2,1,0:T(8,128)S(1)} %get-tuple-element.49), channel_id=1, source_target_pairs={{0,8},{8,0},{16,24},{24,16},{1,9},{9,1},{17,25},{25,17},{2,10},{10... | collective-permute-start | bytes 516104 | tf_op jit(solution)/shard_map/ppermute | solution.py:693
  56.4 0.6 collective-permute-start.8
  57.0 1.8 %collective-permute-start.9 = (f32[42,8,128]{2,1,0:T(8,128)S(1)}, f32[42,8,128]{2,1,0:T(8,128)S(1)}, u32[]{:S(2)}, u32[]{:S(2)}) collective-permute-start(f32[42,8,128]{2,1,0:T(8,128)S(1)} %get-tuple-element.51), channel_id=1, source_target_pairs={{0,24},{8,16},{16,8},{24,0},{1,25},{9,17},{17,9},{25,1},{2,26},{10... | collective-permute-start | bytes 516104 | tf_op jit(solution)/shard_map/ppermute | solution.py:693
  58.9 2.4 %react.3 = (f32[26,8,128]{2,1,0:T(8,128)S(1)}, f32[26,8,128]{2,1,0:T(8,128)S(1)}, f32[26,8,128]{2,1,0:T(8,128)S(1)}, f32[26,8,128]{2,1,0:T(8,128)S(1)}) custom-call(s32[1]{0:T(128)} %bitcast.place_ref, f32[32,32]{1,0:T(8,128)S(1)} %copy-done.3, f32[32]{0:T(128)S(1)} %copy-done.6, f32[32]{0:T(128)S(1)} %copy-done.7, f32[32]{0:T(128)S(1)} %cosine_add_fusion.surface_ref, ...), custom_call_target="tpu_custom_call" | custom-call | tf_op jit(solution)/shard_map/react/pallas_call | solution.py:505
  61.3 1.1 %collective-permute-start.16 = (f32[26,8,128]{2,1,0:T(8,128)S(1)}, f32[26,8,128]{2,1,0:T(8,128)S(1)}, u32[]{:S(2)}, u32[]{:S(2)}) collective-permute-start(f32[26,8,128]{2,1,0:T(8,128)S(1)} %get-tuple-element.60), channel_id=1, source_target_pairs={{0,8},{8,0},{16,24},{24,16},{1,9},{9,1},{17,25},{25,17},{2,10},{10... | collective-permute-start | bytes 319496 | tf_op jit(solution)/shard_map/ppermute | solution.py:693
  62.5 1.6 %collective-permute-start.17 = (f32[26,8,128]{2,1,0:T(8,128)S(1)}, f32[26,8,128]{2,1,0:T(8,128)S(1)}, u32[]{:S(2)}, u32[]{:S(2)}) collective-permute-start(f32[26,8,128]{2,1,0:T(8,128)S(1)} %get-tuple-element.61), channel_id=1, source_target_pairs={{0,16},{8,24},{16,0},{24,8},{1,17},{9,25},{17,1},{25,9},{2,18},{10... | collective-permute-start | bytes 319496 | tf_op jit(solution)/shard_map/ppermute | solution.py:693
  64.1 6.8 %collective-permute-done.16.refs_5_ = f32[26,8,128]{2,1,0:T(8,128)S(1)} collective-permute-done((f32[26,8,128]{2,1,0:T(8,128)S(1)}, f32[26,8,128]{2,1,0:T(8,128)S(1)}, u32[]{:S(2)}, u32[]{:S(2)}) %collective-permute-start.16) | collective-permute-done | bytes 106528 | tf_op jit(solution)/shard_map/ppermute | solution.py:693
  70.9 2.0 %collective-permute-start.18 = (f32[26,8,128]{2,1,0:T(8,128)S(1)}, f32[26,8,128]{2,1,0:T(8,128)S(1)}, u32[]{:S(2)}, u32[]{:S(2)}) collective-permute-start(f32[26,8,128]{2,1,0:T(8,128)S(1)} %get-tuple-element.62), channel_id=1, source_target_pairs={{0,24},{8,16},{16,8},{24,0},{1,25},{9,17},{17,9},{25,1},{2,26},{10... | collective-permute-start | bytes 319496 | tf_op jit(solution)/shard_map/ppermute | solution.py:693
  72.9 4.0 %momentum.1 = (f32[64,128]{1,0:T(8,128)}, f32[64,128]{1,0:T(8,128)}, f32[32,128]{1,0:T(8,128)}) custom-call(s32[1]{0:T(128)} %bitcast.place_ref, f32[36]{0:T(128)S(1)} %sine_multiply_fusion.coriolis_ref, f32[36]{0:T(128)S(1)} %and_convert_fusion.inside_ref, f32[96,8,128]{2,1,0:T(8,128)S(1)} %get-tuple-element.41.flow_ref, ...), custom_call_target="tpu_custom_call" | custom-call | tf_op jit(solution)/shard_map/momentum/pallas_call | solution.py:673
  76.9 5.5 %collective-permute-done.17.refs_6_ = f32[26,8,128]{2,1,0:T(8,128)S(1)} collective-permute-done((f32[26,8,128]{2,1,0:T(8,128)S(1)}, f32[26,8,128]{2,1,0:T(8,128)S(1)}, u32[]{:S(2)}, u32[]{:S(2)}) %collective-permute-start.17) | collective-permute-done | bytes 106528 | tf_op jit(solution)/shard_map/ppermute | solution.py:693
  82.5 1.3 %finish.1 = (f32[8,8,32,128]{3,2,1,0:T(8,128)}, f32[2,32,128]{2,1,0:T(8,128)}) custom-call(s32[1]{0:T(128)} %bitcast.place_ref, f32[2,32,128]{2,1,0:T(8,128)S(1)} %copy-done.4, f32[42,8,128]{2,1,0:T(8,128)S(1)} %get-tuple-element.48.refs_0_, f32[42,8,128]{2,1,0:T(8,128)S(1)} %collective-permute-done.7.refs_1_, ...), custom_call_target="tpu_custom_call" | custom-call | tf_op jit(solution)/shard_map/finish/pallas_call | solution.py:553
  (36 shorter events, 0.5 us)
Async XLA Ops:
  0.6 11.5 %copy-start.2 = (s32[32,128]{1,0:T(8,128)S(1)}, s32[32,128]{1,0:T(8,128)}, u32[]{:S(2)}) copy-start(s32[32,128]{1,0:T(8,128)} %tally_ref.3) | copy-start | bytes 49156
  0.6 11.5 %copy-start.5 = (f32[32,128]{1,0:T(8,128)S(1)}, f32[32,128]{1,0:T(8,128)}, u32[]{:S(2)}) copy-start(f32[32,128]{1,0:T(8,128)} %refs_4_.1) | copy-start | bytes 49156
  1.4 8.0 %collective-permute-start.2 = (f32[2,64,128]{2,1,0:T(8,128)S(1)}, f32[2,64,128]{2,1,0:T(8,128)S(1)}, u32[]{:S(2)}, u32[]{:S(2)}) collective-permute-start(f32[2,64,128]{2,1,0:T(8,128)S(1)} %pad_maximum_fusion.own_ref), channel_id=1, source_target_pairs={{0,24},{8,16},{16,8},{24,0},{1,25},{9,17},{17,9},{25,1},{2,26},{10... | collective-permute-start | bytes 196616 | tf_op jit(solution)/shard_map/ppermute | solution.py:693
  6.5 5.6 %collective-permute-start.1 = (f32[2,64,128]{2,1,0:T(8,128)S(1)}, f32[2,64,128]{2,1,0:T(8,128)S(1)}, u32[]{:S(2)}, u32[]{:S(2)}) collective-permute-start(f32[2,64,128]{2,1,0:T(8,128)S(1)} %pad_maximum_fusion.own_ref), channel_id=1, source_target_pairs={{0,16},{8,24},{16,0},{24,8},{1,17},{9,25},{17,1},{25,9},{2,18},{10... | collective-permute-start | bytes 196616 | tf_op jit(solution)/shard_map/ppermute | solution.py:693
  6.5 5.6 %collective-permute-start = (f32[2,64,128]{2,1,0:T(8,128)S(1)}, f32[2,64,128]{2,1,0:T(8,128)S(1)}, u32[]{:S(2)}, u32[]{:S(2)}) collective-permute-start(f32[2,64,128]{2,1,0:T(8,128)S(1)} %pad_maximum_fusion.own_ref), channel_id=1, source_target_pairs={{0,8},{8,0},{16,24},{24,16},{1,9},{9,1},{17,25},{25,17},{2,10},{10... | collective-permute-start | bytes 196616 | tf_op jit(solution)/shard_map/ppermute | solution.py:693
  7.2 1.2 %copy-start = (f32[8,8,32,128]{3,2,1,0:T(8,128)S(1)}, f32[8,8,32,128]{3,2,1,0:T(8,128)}, u32[]{:S(2)}) copy-start(f32[8,8,32,128]{3,2,1,0:T(8,128)} %param.9) | copy-start | bytes 3145732
  8.4 11.7 %copy-start.1 = (f32[8,8,32,128]{3,2,1,0:T(8,128)S(1)}, f32[8,8,32,128]{3,2,1,0:T(8,128)}, u32[]{:S(2)}) copy-start(f32[8,8,32,128]{3,2,1,0:T(8,128)} %param.9) | copy-start | bytes 3145732
  12.5 16.2 %collective-permute-start.10 = (f32[44,8,128]{2,1,0:T(8,128)S(1)}, f32[44,8,128]{2,1,0:T(8,128)S(1)}, u32[]{:S(2)}, u32[]{:S(2)}) collective-permute-start(f32[44,8,128]{2,1,0:T(8,128)S(1)} %get-tuple-element.52), channel_id=1, source_target_pairs={{0,2},{2,4},{4,6},{1,3},{3,5},{5,7},{8,10},{10,12},{12,14},{9,11},... | collective-permute-start | bytes 540680 | tf_op jit(solution)/shard_map/ppermute | solution.py:705
  14.1 14.6 %collective-permute-start.11 = (f32[44,8,128]{2,1,0:T(8,128)S(1)}, f32[44,8,128]{2,1,0:T(8,128)S(1)}, u32[]{:S(2)}, u32[]{:S(2)}) collective-permute-start(f32[44,8,128]{2,1,0:T(8,128)S(1)} %get-tuple-element.53), channel_id=1, source_target_pairs={{2,0},{4,2},{6,4},{3,1},{5,3},{7,5},{10,8},{12,10},{14,12},{11,9},... | collective-permute-start | bytes 540680 | tf_op jit(solution)/shard_map/ppermute | solution.py:705
  15.4 4.7 %collective-permute-start.3 = (f32[24,8,128]{2,1,0:T(8,128)S(1)}, f32[24,8,128]{2,1,0:T(8,128)S(1)}, u32[]{:S(2)}, u32[]{:S(2)}) collective-permute-start(f32[24,8,128]{2,1,0:T(8,128)S(1)} %get-tuple-element.43), channel_id=1, source_target_pairs={{0,1},{1,0},{2,3},{3,2},{4,5},{5,4},{6,7},{7,6},{8,9},{9,8},{10,11... | collective-permute-start | bytes 294920 | tf_op jit(solution)/shard_map/ppermute | solution.py:712
  27.9 14.5 %collective-permute-start.4 = (f32[40,8,128]{2,1,0:T(8,128)S(1)}, f32[40,8,128]{2,1,0:T(8,128)S(1)}, u32[]{:S(2)}, u32[]{:S(2)}) collective-permute-start(f32[40,8,128]{2,1,0:T(8,128)S(1)} %get-tuple-element.45), channel_id=1, source_target_pairs={{0,8},{8,0},{16,24},{24,16},{1,9},{9,1},{17,25},{25,17},{2,10},{10... | collective-permute-start | bytes 491528 | tf_op jit(solution)/shard_map/ppermute | solution.py:693
  28.9 5.3 %collective-permute-start.12 = (f32[6,8,128]{2,1,0:T(8,128)S(1)}, f32[6,8,128]{2,1,0:T(8,128)S(1)}, u32[]{:S(2)}, u32[]{:S(2)}) collective-permute-start(f32[6,8,128]{2,1,0:T(8,128)S(1)} %pack_edges.1), channel_id=1, source_target_pairs={{0,1},{1,0},{2,3},{3,2},{4,5},{5,4},{6,7},{7,6},{8,9},{9,8},{10,11... | collective-permute-start | bytes 73736 | tf_op jit(solution)/shard_map/ppermute | solution.py:712
  30.5 15.0 %collective-permute-start.5 = (f32[40,8,128]{2,1,0:T(8,128)S(1)}, f32[40,8,128]{2,1,0:T(8,128)S(1)}, u32[]{:S(2)}, u32[]{:S(2)}) collective-permute-start(f32[40,8,128]{2,1,0:T(8,128)S(1)} %get-tuple-element.46), channel_id=1, source_target_pairs={{0,16},{8,24},{16,0},{24,8},{1,17},{9,25},{17,1},{25,9},{2,18},{10... | collective-permute-start | bytes 491528 | tf_op jit(solution)/shard_map/ppermute | solution.py:693
  32.7 12.8 %collective-permute-start.6 = (f32[40,8,128]{2,1,0:T(8,128)S(1)}, f32[40,8,128]{2,1,0:T(8,128)S(1)}, u32[]{:S(2)}, u32[]{:S(2)}) collective-permute-start(f32[40,8,128]{2,1,0:T(8,128)S(1)} %get-tuple-element.47), channel_id=1, source_target_pairs={{0,24},{8,16},{16,8},{24,0},{1,25},{9,17},{17,9},{25,1},{2,26},{10... | collective-permute-start | bytes 491528 | tf_op jit(solution)/shard_map/ppermute | solution.py:693
  34.3 11.3 %copy-start.3 = (f32[32,32]{1,0:T(8,128)S(1)}, f32[32,32]{1,0:T(8,128)}, u32[]{:S(2)}) copy-start(f32[32,32]{1,0:T(8,128)} %table_ref.3) | copy-start | bytes 12292
  39.4 17.6 %collective-permute-start.13 = (f32[24,8,128]{2,1,0:T(8,128)S(1)}, f32[24,8,128]{2,1,0:T(8,128)S(1)}, u32[]{:S(2)}, u32[]{:S(2)}) collective-permute-start(f32[24,8,128]{2,1,0:T(8,128)S(1)} %get-tuple-element.55), channel_id=1, source_target_pairs={{0,8},{8,0},{16,24},{24,16},{1,9},{9,1},{17,25},{25,17},{2,10},{10... | collective-permute-start | bytes 294920 | tf_op jit(solution)/shard_map/ppermute | solution.py:693
  39.5 19.4 %collective-permute-start.14 = (f32[24,8,128]{2,1,0:T(8,128)S(1)}, f32[24,8,128]{2,1,0:T(8,128)S(1)}, u32[]{:S(2)}, u32[]{:S(2)}) collective-permute-start(f32[24,8,128]{2,1,0:T(8,128)S(1)} %get-tuple-element.56), channel_id=1, source_target_pairs={{0,16},{8,24},{16,0},{24,8},{1,17},{9,25},{17,1},{25,9},{2,18},{10... | collective-permute-start | bytes 294920 | tf_op jit(solution)/shard_map/ppermute | solution.py:693
  42.4 16.5 %collective-permute-start.15 = (f32[24,8,128]{2,1,0:T(8,128)S(1)}, f32[24,8,128]{2,1,0:T(8,128)S(1)}, u32[]{:S(2)}, u32[]{:S(2)}) collective-permute-start(f32[24,8,128]{2,1,0:T(8,128)S(1)} %get-tuple-element.57), channel_id=1, source_target_pairs={{0,24},{8,16},{16,8},{24,0},{1,25},{9,17},{17,9},{25,1},{2,26},{10... | collective-permute-start | bytes 294920 | tf_op jit(solution)/shard_map/ppermute | solution.py:693
  44.0 1.6 %copy-start.6 = (f32[32]{0:T(128)S(1)}, f32[32]{0:T(128)}, u32[]{:S(2)}) copy-start(f32[32]{0:T(128)} %pace_ref.3) | copy-start | bytes 388
  44.0 1.6 %copy-start.7 = (f32[32]{0:T(128)S(1)}, f32[32]{0:T(128)}, u32[]{:S(2)}) copy-start(f32[32]{0:T(128)} %uptake_ref.3) | copy-start | bytes 388
  48.2 34.3 %collective-permute-start.7 = (f32[42,8,128]{2,1,0:T(8,128)S(1)}, f32[42,8,128]{2,1,0:T(8,128)S(1)}, u32[]{:S(2)}, u32[]{:S(2)}) collective-permute-start(f32[42,8,128]{2,1,0:T(8,128)S(1)} %get-tuple-element.49), channel_id=1, source_target_pairs={{0,8},{8,0},{16,24},{24,16},{1,9},{9,1},{17,25},{25,17},{2,10},{10... | collective-permute-start | bytes 516104 | tf_op jit(solution)/shard_map/ppermute | solution.py:693
  56.4 26.1 %collective-permute-start.8 = (f32[42,8,128]{2,1,0:T(8,128)S(1)}, f32[42,8,128]{2,1,0:T(8,128)S(1)}, u32[]{:S(2)}, u32[]{:S(2)}) collective-permute-start(f32[42,8,128]{2,1,0:T(8,128)S(1)} %get-tuple-element.50), channel_id=1, source_target_pairs={{0,16},{8,24},{16,0},{24,8},{1,17},{9,25},{17,1},{25,9},{2,18},{10... | collective-permute-start | bytes 516104 | tf_op jit(solution)/shard_map/ppermute | solution.py:693
  57.0 25.4 %collective-permute-start.9 = (f32[42,8,128]{2,1,0:T(8,128)S(1)}, f32[42,8,128]{2,1,0:T(8,128)S(1)}, u32[]{:S(2)}, u32[]{:S(2)}) collective-permute-start(f32[42,8,128]{2,1,0:T(8,128)S(1)} %get-tuple-element.51), channel_id=1, source_target_pairs={{0,24},{8,16},{16,8},{24,0},{1,25},{9,17},{17,9},{25,1},{2,26},{10... | collective-permute-start | bytes 516104 | tf_op jit(solution)/shard_map/ppermute | solution.py:693
  61.3 9.6 %collective-permute-start.16 = (f32[26,8,128]{2,1,0:T(8,128)S(1)}, f32[26,8,128]{2,1,0:T(8,128)S(1)}, u32[]{:S(2)}, u32[]{:S(2)}) collective-permute-start(f32[26,8,128]{2,1,0:T(8,128)S(1)} %get-tuple-element.60), channel_id=1, source_target_pairs={{0,8},{8,0},{16,24},{24,16},{1,9},{9,1},{17,25},{25,17},{2,10},{10... | collective-permute-start | bytes 319496 | tf_op jit(solution)/shard_map/ppermute | solution.py:693
  62.5 20.0 %collective-permute-start.17 = (f32[26,8,128]{2,1,0:T(8,128)S(1)}, f32[26,8,128]{2,1,0:T(8,128)S(1)}, u32[]{:S(2)}, u32[]{:S(2)}) collective-permute-start(f32[26,8,128]{2,1,0:T(8,128)S(1)} %get-tuple-element.61), channel_id=1, source_target_pairs={{0,16},{8,24},{16,0},{24,8},{1,17},{9,25},{17,1},{25,9},{2,18},{10... | collective-permute-start | bytes 319496 | tf_op jit(solution)/shard_map/ppermute | solution.py:693
  70.9 11.6 %collective-permute-start.18 = (f32[26,8,128]{2,1,0:T(8,128)S(1)}, f32[26,8,128]{2,1,0:T(8,128)S(1)}, u32[]{:S(2)}, u32[]{:S(2)}) collective-permute-start(f32[26,8,128]{2,1,0:T(8,128)S(1)} %get-tuple-element.62), channel_id=1, source_target_pairs={{0,24},{8,16},{16,8},{24,0},{1,25},{9,17},{17,9},{25,1},{2,26},{10... | collective-permute-start | bytes 319496 | tf_op jit(solution)/shard_map/ppermute | solution.py:693
  72.9 9.6 %copy-start.4 = (f32[2,32,128]{2,1,0:T(8,128)S(1)}, f32[2,32,128]{2,1,0:T(8,128)}, u32[]{:S(2)}) copy-start(f32[2,32,128]{2,1,0:T(8,128)} %thermal_ref.1) | copy-start | bytes 98308
